TPU v7x, 768 devices: a whole 4x8x12 slice. The times are simulated.
768 devices in a mesh: space: 192 (over y, z, core), traj: 4 (over x).
Axes of the slice: x: 4, y: 8, z: 12, core: 2. Of those that a mesh axis runs over, the one named last changes fastest.
Arguments:
- field: float32 [4, 39, 1536, 256], P('traj', None, 'space'), may hold values from -6 to 6
- solid: int32 [4, 1536, 256], P('traj', 'space'), may hold values 0 or 1
- cotangent: float32 [4, 39, 1536, 256], P('traj', None, 'space'), may hold values from -6 to 6
- w_in: bfloat16 [20, 512], replicated, may hold values from -1.25 to 1.25
- b_in: float32 [512], replicated, may hold values from -3 to 3
- w_out: bfloat16 [512, 39], replicated, may hold values from -0.25 to 0.25
- b_out: float32 [39], replicated, may hold values from -3 to 3
Outputs:
- d_field: float32 [4, 39, 1536, 256], P('traj', None, 'space')
- g_w_in: float32 [20, 512], replicated
- g_b_in: float32 [512], replicated
- g_w_out: float32 [512, 39], replicated
- g_b_out: float32 [39], replicated
All inputs are finite; a program needn't handle non-finite values. No bound on the sum of `solid` on one device may be relied on, other than what follows from the above.
Results may differ from a plain program's by a relative error of at most 0.0089.
Values sent between devices are 32-bit elements; how exact they have to be, the bound alone decides.
A program may use at most 32 MiB of HBM per device.

v0:
```python
import math

import jax
import jax.numpy as jnp
from jax import lax
from jax.sharding import PartitionSpec as P

STEPS = 3
NX = 16
NY = 16


def padded_2(shard, sides, width):
    for axis, dim in sides:
        size, length = (lax.axis_size(axis), shard.shape[dim])
        up = [(i, (i + 1) % size) for i in range(size)]
        down = [(j, i) for i, j in up]
        last = lax.slice_in_dim(shard, length - width, length, axis=dim)
        first = lax.slice_in_dim(shard, 0, width, axis=dim)
        before = lax.ppermute(last, axis, up)
        after = lax.ppermute(first, axis, down)
        shard = jnp.concatenate([before, shard, after], axis=dim)
    return shard


def velocity_table():
    rows = [(0, 0, 0)]
    for axis_one in range(3):
        for sign in (1, -1):
            entry = [0, 0, 0]
            entry[axis_one] = sign
            rows.append(tuple(entry))
    for along_x in (1, -1):
        for along_y in (1, -1):
            for along_z in (1, -1):
                rows.append((along_x, along_y, along_z))
    for axis_one in range(3):
        for sign in (1, -1):
            entry = [0, 0, 0]
            entry[axis_one] = 2 * sign
            rows.append(tuple(entry))
    for first, second in ((0, 1), (0, 2), (1, 2)):
        for sign_one in (2, -2):
            for sign_two in (2, -2):
                entry = [0, 0, 0]
                entry[first] = sign_one
                entry[second] = sign_two
                rows.append(tuple(entry))
    for axis_one in range(3):
        for sign in (1, -1):
            entry = [0, 0, 0]
            entry[axis_one] = 3 * sign
            rows.append(tuple(entry))
    return rows


def opposite_index(velocity):
    result = []
    for row in velocity:
        flipped = (-row[0], -row[1], -row[2])
        result.append(velocity.index(flipped))
    return result


def hermite_table(velocity):
    sound = 2.0 / 3.0
    ident = [[1.0 if a == b else 0.0 for b in range(3)] for a in range(3)]
    speed = [[float(v) for v in row] for row in velocity]
    rows = [[1.0 for row in speed]]
    for first in range(3):
        rows.append([row[first] for row in speed])
    for first in range(3):
        for second in range(first, 3):
            rows.append([row[first] * row[second] - sound * ident[first][second] for row in speed])
    for first in range(3):
        for second in range(first, 3):
            for third in range(second, 3):
                rows.append(
                    [
                        row[first] * row[second] * row[third]
                        - sound
                        * (
                            row[first] * ident[second][third]
                            + row[second] * ident[first][third]
                            + row[third] * ident[first][second]
                        )
                        for row in speed
                    ]
                )
    normed = []
    for values in rows:
        length = math.sqrt(sum((v * v for v in values)))
        normed.append([v / length for v in values])
    return jnp.asarray(normed, jnp.float32)


def collide_block(block, weights, hermite):
    w_in, b_in, w_out, b_out = weights
    moments = jnp.dot(
        hermite, block, precision=lax.Precision.HIGHEST, preferred_element_type=jnp.float32
    )
    rounded = moments.astype(jnp.bfloat16)
    hidden = jnp.tanh(
        jnp.dot(w_in.T, rounded, preferred_element_type=jnp.float32) + b_in[:, None]
    ).astype(jnp.bfloat16)
    change = jnp.dot(w_out.T, hidden, preferred_element_type=jnp.float32) + b_out[:, None]
    return (block + change, rounded, hidden)


def adjoint_block(block, incoming, weights, hermite):
    w_in, b_in, w_out, b_out = weights
    unused, rounded, hidden = collide_block(block, weights, hermite)
    grad_rounded = incoming.astype(jnp.bfloat16)
    d_hidden = jnp.dot(w_out, grad_rounded, preferred_element_type=jnp.float32)
    hidden_wide = hidden.astype(jnp.float32)
    d_act = (d_hidden * (1.0 - hidden_wide * hidden_wide)).astype(jnp.bfloat16)
    d_moments = jnp.dot(w_in, d_act, preferred_element_type=jnp.float32)
    d_block = incoming + jnp.dot(
        hermite.T, d_moments, precision=lax.Precision.HIGHEST, preferred_element_type=jnp.float32
    )
    grads = (
        jnp.dot(rounded, d_act.T, preferred_element_type=jnp.float32),
        jnp.sum(d_act.astype(jnp.float32), axis=1),
        jnp.dot(hidden, grad_rounded.T, preferred_element_type=jnp.float32),
        jnp.sum(incoming, axis=1),
    )
    return (d_block, grads)


def collide_layers(state, weights, hermite):
    layers = jnp.moveaxis(state, 1, 0)
    result = lax.map(lambda layer: collide_block(layer, weights, hermite)[0], layers)
    return jnp.moveaxis(result, 0, 1)


def adjoint_layers(state, incoming, weights, hermite):
    zeros = tuple((jnp.zeros(w.shape, jnp.float32) for w in weights))

    def advance(totals, pair):
        d_layer, grads = adjoint_block(pair[0], pair[1], weights, hermite)
        return (tuple((a + b for a, b in zip(totals, grads))), d_layer)

    totals, layers = lax.scan(
        advance, zeros, (jnp.moveaxis(state, 1, 0), jnp.moveaxis(incoming, 1, 0))
    )
    return (jnp.moveaxis(layers, 0, 1), totals)


def roll_plane(rows, along_x, along_y):
    depth = rows.shape[0]
    grid = rows.reshape(depth, NX, NY)
    return jnp.roll(grid, (along_x, along_y), (1, 2)).reshape(depth, NX * NY)


def stream_local(state, velocity, sign):
    depth = state.shape[1]
    count = len(velocity)
    moves = [-sign * velocity[index][2] for index in range(count)]
    pieces = []
    padded = padded_2(state, (("space", 1),), 3)
    for index in range(count):
        pieces.append(padded[index, 3 + moves[index] : 3 + moves[index] + depth])
    moved = []
    for index in range(count):
        moved.append(
            roll_plane(pieces[index], sign * velocity[index][0], sign * velocity[index][1])
        )
    return jnp.stack(moved)


def per_device(field, solid, cotangent, w_in, b_in, w_out, b_out):
    velocity = velocity_table()
    opposite = jnp.asarray(opposite_index(velocity), jnp.int32)
    hermite = hermite_table(velocity)
    weights = (w_in, b_in, w_out, b_out)
    local_count, pops, depth, plane = field.shape
    walls = [solid[0].astype(jnp.float32)[None]]
    current = [field[0]]
    states = [[]]
    for step in range(STEPS):
        t = 0
        states[t].append(current[t])
        post = collide_layers(current[t], weights, hermite)
        current[t] = (1.0 - walls[t]) * stream_local(post, velocity, 1) + walls[t] * post[opposite]
    totals = tuple((jnp.zeros(w.shape, jnp.float32) for w in weights))
    backs = [cotangent[0]]
    for step in range(STEPS - 1, -1, -1):
        local_sums = tuple((jnp.zeros(w.shape, jnp.float32) for w in weights))
        t = 0
        incoming = (
            stream_local((1.0 - walls[t]) * backs[t], velocity, -1)
            + (walls[t] * backs[t])[opposite]
        )
        backs[t], grads = adjoint_layers(states[t][step], incoming, weights, hermite)
        local_sums = tuple((b for b in grads))
        totals = tuple((a + b for a, b in zip(totals, local_sums)))
    totals = lax.psum((totals[0], totals[1], totals[2], totals[3]), ("space", "traj"))
    cells = lax.axis_size("traj") * local_count * lax.axis_size("space") * depth * plane * STEPS
    scale = 1.0 / math.sqrt(float(cells))
    return (
        jnp.stack(backs),
        totals[0] * scale,
        totals[1] * scale,
        totals[2] * scale,
        totals[3] * scale,
    )


def solution(mesh):
    return jax.shard_map(
        per_device,
        mesh=mesh,
        in_specs=(
            P("traj", None, "space", None),
            P("traj", "space", None),
            P("traj", None, "space", None),
            P(),
            P(),
            P(),
            P(),
        ),
        out_specs=(P("traj", None, "space", None), P(), P(), P(), P()),
        check_vma=False,
    )
```

profile of v0, /device:TPU:1, one launch (start us, length us, event | category | flops | bytes accessed | tf_op | source)
XLA Modules:
  0.0 729.3 jit_solution(5169670671536981982)
XLA Ops:
  9.1 20.9 %while.82 = (s32[]{:T(128)}, f32[8,39,256]{2,0,1:T(8,128)S(1)}, f32[8,39,256]{2,1,0:T(8,128)S(1)}, bf16[20,512]{1,0:T(8,128)(2,1)S(1)}, f32[512]{0:T(512)S(1)}, ...) while((s32[]{:T(128)}, f32[8,39,256]{2,0,1:T(8,128)S(1)}, ...), condition=%wide.region_1.2_spmd.clone, body=%wide.region_0.1_spmd.sunk.clone.sunk | while | flops 18149888 | bytes 376077 | solution.py:132
  15.1 1.8 dynamic_update_slice.34
  23.0 1.8 dynamic_update_slice.34
  30.0 5.4 collective-permute-start
  35.4 8.9 %collective-permute-start.1 = (f32[39,3,256]{2,1,0:T(4,128)S(1)}, f32[39,3,256]{2,1,0:T(4,128)S(1)}, u32[]{:S(2)}, u32[]{:S(2)}) collective-permute-start(f32[39,3,256]{2,1,0:T(4,128)S(1)} %get-tuple-element.912), channel_id=1, source_target_pairs={{4,0},{8,4},{12,8},{16,12},{20,16},{24,20},{28,24},{32,28},{36,32}... | collective-permute-start | bytes 359432 | tf_op jit(solution)/shard_map/ppermute | solution.py:21
  57.6 20.9 %while.83 = (s32[]{:T(128)}, f32[8,39,256]{2,0,1:T(8,128)S(1)}, f32[8,39,256]{2,1,0:T(8,128)S(1)}, bf16[20,512]{1,0:T(8,128)(2,1)S(1)}, f32[512]{0:T(512)S(1)}, ...) while((s32[]{:T(128)}, f32[8,39,256]{2,0,1:T(8,128)S(1)}, ...), condition=%wide.region_3.4_spmd.clone, body=%wide.region_2.3_spmd.sunk.clone.sunk | while | flops 18149888 | bytes 376077 | solution.py:132
  58.4 1.8 dynamic_update_slice.35
  61.0 1.8 dynamic_update_slice.35
  63.6 1.8 dynamic_update_slice.35
  66.2 1.8 dynamic_update_slice.35
  71.4 1.8 dynamic_update_slice.35
  74.1 1.8 dynamic_update_slice.35
  79.7 1.9 collective-permute-start.2
  81.6 8.1 %collective-permute-start.3 = (f32[39,3,256]{2,1,0:T(4,128)S(1)}, f32[39,3,256]{2,1,0:T(4,128)S(1)}, u32[]{:S(2)}, u32[]{:S(2)}) collective-permute-start(f32[39,3,256]{2,1,0:T(4,128)S(1)} %get-tuple-element.893), channel_id=1, source_target_pairs={{4,0},{8,4},{12,8},{16,12},{20,16},{24,20},{28,24},{32,28},{36,32}... | collective-permute-start | bytes 359432 | tf_op jit(solution)/shard_map/ppermute | solution.py:21
  102.6 8.7 %collective-permute-start.4 = (f32[39,3,256]{2,1,0:T(4,128)S(1)}, f32[39,3,256]{2,1,0:T(4,128)S(1)}, u32[]{:S(2)}, u32[]{:S(2)}) collective-permute-start(f32[39,3,256]{2,1,0:T(4,128)S(1)} %get-tuple-element.875), channel_id=1, source_target_pairs={{4,0},{8,4},{12,8},{16,12},{20,16},{24,20},{28,24},{32,28},{36,32}... | collective-permute-start | bytes 359432 | tf_op jit(solution)/shard_map/ppermute | solution.py:21
  111.3 1.9 collective-permute-start.5
  113.9 5.4 collective-permute-done.5
  129.1 30.4 %while.84 = (s32[]{:T(128)}, f32[20,512]{1,0:T(8,128)S(1)}, f32[512]{0:T(512)S(1)}, f32[512,39]{0,1:T(8,128)S(1)}, f32[39]{0:T(128)S(1)}, /*index=5*/f32[8,39,25...) while((s32[]{:T(128)}, f32[20,512]{1,0:T(8,128)S(1)}, ...), condition=%wide.region_7.8_spmd.clone.clone, body=%wide.region_4.7_spmd.sunk.clone.clone.sunk | while | flops 42233896 | bytes 2503530 | solution.py:143
  134.6 1.8 dynamic_update_slice.36
  138.4 1.8 dynamic_update_slice.36
  149.8 1.8 dynamic_update_slice.36
  153.5 1.8 dynamic_update_slice.36
  160.8 9.0 %collective-permute-start.6 = (f32[39,3,256]{2,1,0:T(4,128)S(1)}, f32[39,3,256]{2,1,0:T(4,128)S(1)}, u32[]{:S(2)}, u32[]{:S(2)}) collective-permute-start(f32[39,3,256]{2,1,0:T(4,128)S(1)} %get-tuple-element.854), channel_id=1, source_target_pairs={{4,0},{8,4},{12,8},{16,12},{20,16},{24,20},{28,24},{32,28},{36,32}... | collective-permute-start | bytes 359432 | tf_op jit(solution)/shard_map/ppermute | solution.py:21
  169.8 2.1 collective-permute-start.7
  183.8 30.4 %while.85 = (s32[]{:T(128)}, f32[20,512]{1,0:T(8,128)S(1)}, f32[512]{0:T(512)S(1)}, f32[512,39]{0,1:T(8,128)S(1)}, f32[39]{0:T(128)S(1)}, /*index=5*/f32[8,39,25...) while((s32[]{:T(128)}, f32[20,512]{1,0:T(8,128)S(1)}, ...), condition=%wide.region_11.12_spmd.clone.clone, body=%wide.region_8.11_spmd.sunk.clone.clone.sunk | while | flops 42233896 | bytes 2433854 | solution.py:143
  185.4 1.8 dynamic_update_slice.37
  196.8 1.8 dynamic_update_slice.37
  215.4 7.7 %collective-permute-start.8 = (f32[39,3,256]{2,1,0:T(4,128)S(1)}, f32[39,3,256]{2,1,0:T(4,128)S(1)}, u32[]{:S(2)}, u32[]{:S(2)}) collective-permute-start(f32[39,3,256]{2,1,0:T(4,128)S(1)} %get-tuple-element.833), channel_id=1, source_target_pairs={{4,0},{8,4},{12,8},{16,12},{20,16},{24,20},{28,24},{32,28},{36,32}... | collective-permute-start | bytes 359432 | tf_op jit(solution)/shard_map/ppermute | solution.py:21
  223.1 1.9 collective-permute-start.9
  237.1 30.4 %while.86 = (s32[]{:T(128)}, f32[20,512]{1,0:T(8,128)S(1)}, f32[512]{0:T(512)S(1)}, f32[512,39]{0,1:T(8,128)S(1)}, f32[39]{0:T(128)S(1)}, /*index=5*/f32[8,39,25...) while((s32[]{:T(128)}, f32[20,512]{1,0:T(8,128)S(1)}, ...), condition=%wide.region_15.16_spmd.clone.clone, body=%wide.region_12.15_spmd.sunk.clone.clone.sunk | while | flops 42233896 | bytes 2433854 | solution.py:143
  268.3 110.4 %all-reduce = (f32[20,512]{1,0:T(8,128)S(1)}, f32[512]{0:T(512)S(1)}, f32[39]{0:T(128)S(1)}) all-reduce(f32[20,512]{1,0:T(8,128)S(1)} %add_add_fusion.1, f32[512]{0:T(512)S(1)} %add_add_fusion.2, f32[39]{0:T(128)S(1)} %add_add_fusion.3), channel_id=1, replica_groups=mesh['space'=192,'traj'=4] {'space','traj'}, use_global_device_ids=true, to_apply=%region_16.17 | all-reduce | flops 10791 | bytes 86328 | tf_op jit(solution)/shard_map/psum | solution.py:197
  380.4 340.5 %all-reduce.3.cloned.1.call-done = f32[512,39]{0,1:T(8,128)} async-done(((f32[512,39]{0,1:T(8,128)}), f32[512,39]{0,1:T(8,128)}) %all-reduce.3.cloned.1.call-update) | async-done | bytes 79888 | tf_op jit(solution)/shard_map/psum | solution.py:197
  (1364 shorter events, 168.8 us)
Async XLA Ops:
  7.2 713.8 %all-reduce.3.cloned.1.call-start = ((), (), s32[]{:S(2)}) async-start(), calls=%async_computation | async-start | bytes 163840 | tf_op jit(solution)/shard_map/psum | solution.py:197
  8.3 0.7 copy-start
  8.3 0.7 copy-start.1
  8.3 0.8 copy-start.6
  8.3 0.8 copy-start.7
  8.3 0.8 copy-start.8
  30.0 17.6 %collective-permute-start = (f32[39,3,256]{2,1,0:T(4,128)S(1)}, f32[39,3,256]{2,1,0:T(4,128)S(1)}, u32[]{:S(2)}, u32[]{:S(2)}) collective-permute-start(f32[39,3,256]{2,1,0:T(4,128)S(1)} %get-tuple-element.913), channel_id=1, source_target_pairs={{0,4},{4,8},{8,12},{12,16},{16,20},{20,24},{24,28},{28,32},{32,36}... | collective-permute-start | bytes 359432 | tf_op jit(solution)/shard_map/ppermute | solution.py:20
  35.4 12.3 %collective-permute-start.1 = (f32[39,3,256]{2,1,0:T(4,128)S(1)}, f32[39,3,256]{2,1,0:T(4,128)S(1)}, u32[]{:S(2)}, u32[]{:S(2)}) collective-permute-start(f32[39,3,256]{2,1,0:T(4,128)S(1)} %get-tuple-element.912), channel_id=1, source_target_pairs={{4,0},{8,4},{12,8},{16,12},{20,16},{24,20},{28,24},{32,28},{36,32}... | collective-permute-start | bytes 359432 | tf_op jit(solution)/shard_map/ppermute | solution.py:21
  44.5 0.7 copy-start.4
  46.3 0.7 copy-start.5
  79.7 10.7 %collective-permute-start.2 = (f32[39,3,256]{2,1,0:T(4,128)S(1)}, f32[39,3,256]{2,1,0:T(4,128)S(1)}, u32[]{:S(2)}, u32[]{:S(2)}) collective-permute-start(f32[39,3,256]{2,1,0:T(4,128)S(1)} %get-tuple-element.894), channel_id=1, source_target_pairs={{0,4},{4,8},{8,12},{12,16},{16,20},{20,24},{24,28},{28,32},{32,36}... | collective-permute-start | bytes 359432 | tf_op jit(solution)/shard_map/ppermute | solution.py:20
  81.6 9.0 %collective-permute-start.3 = (f32[39,3,256]{2,1,0:T(4,128)S(1)}, f32[39,3,256]{2,1,0:T(4,128)S(1)}, u32[]{:S(2)}, u32[]{:S(2)}) collective-permute-start(f32[39,3,256]{2,1,0:T(4,128)S(1)} %get-tuple-element.893), channel_id=1, source_target_pairs={{4,0},{8,4},{12,8},{16,12},{20,16},{24,20},{28,24},{32,28},{36,32}... | collective-permute-start | bytes 359432 | tf_op jit(solution)/shard_map/ppermute | solution.py:21
  100.3 1.0 copy-start.3
  102.6 11.3 %collective-permute-start.4 = (f32[39,3,256]{2,1,0:T(4,128)S(1)}, f32[39,3,256]{2,1,0:T(4,128)S(1)}, u32[]{:S(2)}, u32[]{:S(2)}) collective-permute-start(f32[39,3,256]{2,1,0:T(4,128)S(1)} %get-tuple-element.875), channel_id=1, source_target_pairs={{4,0},{8,4},{12,8},{16,12},{20,16},{24,20},{28,24},{32,28},{36,32}... | collective-permute-start | bytes 359432 | tf_op jit(solution)/shard_map/ppermute | solution.py:21
  111.3 8.0 %collective-permute-start.5 = (f32[39,3,256]{2,1,0:T(4,128)S(1)}, f32[39,3,256]{2,1,0:T(4,128)S(1)}, u32[]{:S(2)}, u32[]{:S(2)}) collective-permute-start(f32[39,3,256]{2,1,0:T(4,128)S(1)} %get-tuple-element.874), channel_id=1, source_target_pairs={{0,4},{4,8},{8,12},{12,16},{16,20},{20,24},{24,28},{28,32},{32,36}... | collective-permute-start | bytes 359432 | tf_op jit(solution)/shard_map/ppermute | solution.py:20
  160.8 11.8 %collective-permute-start.6 = (f32[39,3,256]{2,1,0:T(4,128)S(1)}, f32[39,3,256]{2,1,0:T(4,128)S(1)}, u32[]{:S(2)}, u32[]{:S(2)}) collective-permute-start(f32[39,3,256]{2,1,0:T(4,128)S(1)} %get-tuple-element.854), channel_id=1, source_target_pairs={{4,0},{8,4},{12,8},{16,12},{20,16},{24,20},{28,24},{32,28},{36,32}... | collective-permute-start | bytes 359432 | tf_op jit(solution)/shard_map/ppermute | solution.py:21
  169.8 4.1 collective-permute-start.7
  215.4 10.3 %collective-permute-start.8 = (f32[39,3,256]{2,1,0:T(4,128)S(1)}, f32[39,3,256]{2,1,0:T(4,128)S(1)}, u32[]{:S(2)}, u32[]{:S(2)}) collective-permute-start(f32[39,3,256]{2,1,0:T(4,128)S(1)} %get-tuple-element.833), channel_id=1, source_target_pairs={{4,0},{8,4},{12,8},{16,12},{20,16},{24,20},{28,24},{32,28},{36,32}... | collective-permute-start | bytes 359432 | tf_op jit(solution)/shard_map/ppermute | solution.py:21
  223.1 4.1 collective-permute-start.9
  267.4 0.8 copy-start.2
Sparse Core Ops, SparseCore 0:
  268.3 452.5 all-reduce.2
where the time goes:
time: 730 us; the launch traced here: 729 us
  waiting for transfers between devices  349 us (48%)
  local copies, waits for them, and re-layouts  112 us (15%)
  blocking collectives  110 us (15%)
  starting transfers between devices  55.9 us (8%)
  matrix products  47.5 us (7%)
  other arithmetic  31.2 us (4%)
  between operations  20.8 us (3%)
    psum x1, waiting for transfers between devices, per_device(): lax.psum((totals[0], totals[1], totals[2], totals[3]), ('space', 'traj'))  341 us
    psum x1, blocking collectives, per_device(): lax.psum((totals[0], totals[1], totals[2], totals[3]), ('space', 'traj'))  110 us
    dynamic_update_slice x80, local copies, waits for them, and re-layouts, collide_layers(): lax.map(lambda layer: collide_block(layer, weights, hermite)[0], layers)  72.8 us
    ppermute x5, starting transfers between devices, padded_2(): after = lax.ppermute(first, axis, down)  42.5 us
    concatenate x220, other arithmetic, roll_plane(): return jnp.roll(grid, (along_x, along_y), (1, 2)).reshape(depth, NX * NY)  16.6 us
  transfers between devices with their start and end apart: 11, of which 5 were waited for; matrix products, arithmetic and copies ran while one was open for 1% of the time, Pallas kernels for 0%

commit v1 on v0

v1 whole, which is shorter than its diff:
```python
import math

import jax
import jax.numpy as jnp
import numpy as np
from jax import lax
from jax.experimental import pallas as pl
from jax.experimental.pallas import tpu as pltpu
from jax.sharding import PartitionSpec as P

STEPS = 3
Q = 39
MOM = 20
HID = 512
CZ = 8
PLANE = 256
ROWS = 40
CELLS = CZ * PLANE
MESH = pl.DeviceIdType.MESH
F32 = jnp.float32
BF16 = jnp.bfloat16
NT = (((1,), (1,)), ((), ()))


def velocity_table():
    rows = [(0, 0, 0)]
    for axis_one in range(3):
        for sign in (1, -1):
            entry = [0, 0, 0]
            entry[axis_one] = sign
            rows.append(tuple(entry))
    for along_x in (1, -1):
        for along_y in (1, -1):
            for along_z in (1, -1):
                rows.append((along_x, along_y, along_z))
    for axis_one in range(3):
        for sign in (1, -1):
            entry = [0, 0, 0]
            entry[axis_one] = 2 * sign
            rows.append(tuple(entry))
    for first, second in ((0, 1), (0, 2), (1, 2)):
        for sign_one in (2, -2):
            for sign_two in (2, -2):
                entry = [0, 0, 0]
                entry[first] = sign_one
                entry[second] = sign_two
                rows.append(tuple(entry))
    for axis_one in range(3):
        for sign in (1, -1):
            entry = [0, 0, 0]
            entry[axis_one] = 3 * sign
            rows.append(tuple(entry))
    return rows


def hermite_table(velocity):
    sound = 2.0 / 3.0
    e = np.asarray(velocity, np.float64)
    ident = np.eye(3)
    rows = [np.ones(len(velocity))]
    for a in range(3):
        rows.append(e[:, a])
    for a in range(3):
        for b in range(a, 3):
            rows.append(e[:, a] * e[:, b] - sound * ident[a, b])
    for a in range(3):
        for b in range(a, 3):
            for c in range(b, 3):
                rows.append(
                    e[:, a] * e[:, b] * e[:, c]
                    - sound * (e[:, a] * ident[b, c] + e[:, b] * ident[a, c] + e[:, c] * ident[a, b])
                )
    return np.stack([r / np.sqrt((r * r).sum()) for r in rows]).astype(np.float32)


def row_order(velocity):
    up = [(0, 0, 3), (0, 0, 2), (2, 0, 2), (-2, 0, 2), (0, 2, 2), (0, -2, 2), (0, 0, 1), (1, 1, 1)]
    mixed = [(1, -1, 1), (-1, 1, 1), (-1, -1, 1), (1, 0, 0)]
    level = [(0, 1, 0), (2, 0, 0), (0, 2, 0), (2, 2, 0), (2, -2, 0), (3, 0, 0), (0, 3, 0)]
    neg = lambda group: [tuple(-v for v in e) for e in group]
    order = up + mixed + neg(mixed) + neg(up) + level + [(0, 0, 0)] + neg(level)
    assert sorted(order) == sorted(velocity)
    return order


def tables():
    velocity = velocity_table()
    order = row_order(velocity)
    where = [velocity.index(e) for e in order]
    herm = hermite_table(velocity)[:, where]
    herm = np.concatenate([herm, np.zeros((MOM, 1), np.float32)], axis=1)
    bf = lambda a: np.asarray(jnp.asarray(a).astype(BF16).astype(F32))
    hi = bf(herm)
    mid = bf(herm - hi)
    low = bf(herm - hi - mid)
    thick = np.concatenate([hi, mid, low, np.zeros((4, ROWS), np.float32)])
    spread = np.zeros((64, 128), np.float32)
    for part in range(3):
        spread[:, part * ROWS : (part + 1) * ROWS] = thick
    for part in range(3):
        spread[60 + part, 120 + part] = 1.0
    final = np.zeros((24, 128), np.float32)
    final[:MOM, :ROWS] = herm
    final[:MOM, ROWS : 2 * ROWS] = herm
    final[MOM, 120] = 1.0
    pick = np.zeros((48, 128), np.float32)
    for row, q in enumerate(where):
        pick[row, q] = 1.0
    floats = np.zeros((320, 128), np.float32)
    floats[0:64] = spread
    floats[64:88] = final
    floats[88:136] = pick
    floats[136:184, :48] = pick.T[:48, :48]
    floats[184:224, :64] = thick.T
    ints = np.zeros((4, ROWS, 128), np.int32)
    for row, e in enumerate(order):
        for back, sign in ((0, 1), (1, -1)):
            for lane in range(128):
                x, y = lane // 16, lane % 16
                source = ((x - sign * e[0]) % 16) * 16 + (y - sign * e[1]) % 16
                ints[2 * back, row, lane] = source % 128
                ints[2 * back + 1, row, lane] = source // 128
    ints[0, 39], ints[2, 39] = np.arange(128), np.arange(128)
    return where, floats, ints


WHERE, FLOATS, INTS = tables()


def kernel(
    grid, scale, field, solid, cotangent, w_in, b_in, w_out, b_out, floats, ints, d_field, sums,
    pads, start, back_in, state, bounce, walls, xs, hid, dact, gbs, w_stack, w_trans, wo, wo_trans, bias, acc_in, acc_out,
    acc_b, parts, from_core, from_y, from_x, from_z, merged, final,
    halo_send, halo_recv, core_send, core_recv, y_send, y_recv, x_send, x_recv, z_send, z_recv, e_send, e_recv,
):
    ny, nz, nx = grid
    me_s, me_x = lax.axis_index("space"), lax.axis_index("traj")
    core = lax.rem(me_s, 2)
    me_z = lax.rem(me_s // 2, nz)
    me_y = me_s // (2 * nz)
    n_space = ny * nz * 2
    up = (lax.rem(me_s + 1, n_space), me_x)
    down = (lax.rem(me_s + n_space - 1, n_space), me_x)
    place = lambda y, z, c: (y * nz + z) * 2 + c
    partner = (place(me_y, me_z, 1 - core), me_x)
    at_y = lambda k: (place(lax.rem(me_y + k, ny), me_z, core), me_x)
    at_z = lambda k: (place(me_y, lax.rem(me_z + k, nz), core), me_x)
    at_x = lambda k: (me_s, lax.rem(me_x + k, nx))
    peers = [up, down] + [at_y(k) for k in range(1, ny)] + [at_x(k) for k in range(1, nx)] + [at_z(k) for k in range(1, nz)]

    barrier = pltpu.get_barrier_semaphore()
    for peer in peers:
        pl.semaphore_signal(barrier, inc=1, device_id=peer, device_id_type=MESH)

    w = w_in[...].astype(F32)
    b = b_in[...]
    b_hi = b.astype(BF16).astype(F32)
    b_mid = (b - b_hi).astype(BF16).astype(F32)
    b_low = b - b_hi - b_mid
    stack = jnp.concatenate([w, w, w, b_hi, b_mid, b_low, jnp.zeros((1, HID), F32)], axis=0)
    spread = floats[0:64, :].astype(BF16)
    full = jnp.dot(stack.T.astype(BF16), spread, preferred_element_type=F32)
    column = lax.broadcasted_iota(jnp.int32, (HID, 128), 1)
    low_part = full - full.astype(BF16).astype(F32)
    w_stack[...] = jnp.where((column >= 2 * ROWS) & (column < 3 * ROWS), low_part, full).astype(BF16)
    thick_t = floats[184:224, 0:64].astype(BF16)
    w_trans[...] = jnp.dot(thick_t, stack.astype(BF16), preferred_element_type=F32).astype(BF16)
    pick = floats[88:136, 0:Q].astype(BF16)
    by_row = jnp.dot(pick, w_out[...], preferred_element_type=F32)
    wo[...] = by_row.T.astype(BF16)
    wo_trans[...] = by_row[:ROWS].astype(BF16)
    bo = lax.dot_general(
        floats[88:136, 0:Q], jnp.broadcast_to(b_out[...], (8, Q)), NT, precision=lax.Precision.HIGHEST, preferred_element_type=F32
    )
    bias[...] = jnp.broadcast_to(bo[:ROWS, 0:1], (ROWS, PLANE))
    acc_b[...] = jnp.zeros((ROWS, PLANE), F32)

    zeros = jnp.zeros((CZ, 128), F32)
    for half in range(2):
        lanes = slice(128 * half, 128 * half + 128)
        for row in range(ROWS):
            if row < Q:
                start[half, pl.ds(row, CZ, stride=ROWS), :] = field[0, WHERE[row], :, lanes]
                back_in[half, pl.ds(row, CZ, stride=ROWS), :] = cotangent[0, WHERE[row], :, lanes]
            else:
                start[half, pl.ds(row, CZ, stride=ROWS), :] = zeros
                back_in[half, pl.ds(row, CZ, stride=ROWS), :] = zeros
    for z in range(CZ):
        walls[z] = jnp.broadcast_to(solid[0, z : z + 1, :], (8, PLANE))

    row8 = lax.broadcasted_iota(jnp.int32, (8, PLANE), 0)

    def wall_of(z):
        return walls[z] > 0

    def opposite(v):
        last = row8 == 7
        return jnp.concatenate(
            [
                v[16:24],
                jnp.concatenate([v[12:16], v[8:12]], axis=0),
                v[0:8],
                jnp.where(last, v[24:32], v[32:40]),
                jnp.where(last, v[32:40], v[24:32]),
            ],
            axis=0,
        )

    def select(wall, a, b):
        return jnp.concatenate([jnp.where(wall, a[8 * i : 8 * i + 8], b[8 * i : 8 * i + 8]) for i in range(5)], axis=0)

    def streamed(pad, z, sign):
        here = z + 3
        plane = lambda by, rows: pad[here - sign * by, rows, :]
        a, m, o, r = slice(0, 8), slice(8, 16), slice(16, 24), slice(24, 40)
        top = jnp.where(row8 == 0, plane(3, a), jnp.where(row8 < 6, plane(2, a), plane(1, a)))
        mix = jnp.where(row8 < 3, plane(1, m), jnp.where((row8 > 3) & (row8 < 7), plane(-1, m), plane(0, m)))
        low = jnp.where(row8 == 0, plane(-3, o), jnp.where(row8 < 6, plane(-2, o), plane(-1, o)))
        v = jnp.concatenate([top, mix, low, plane(0, r)], axis=0)
        which = 0 if sign == 1 else 2
        index, far = ints[which], ints[which + 1] > 0
        left = jnp.take_along_axis(v[:, 0:128], index, axis=1, mode="promise_in_bounds")
        right = jnp.take_along_axis(v[:, 128:256], index, axis=1, mode="promise_in_bounds")
        return jnp.concatenate([jnp.where(far, right, left), jnp.where(far, left, right)], axis=1)

    def cells_of(z):
        return pl.ds(pl.multiple_of(z * PLANE, PLANE), PLANE)

    def loaded(ref, z):
        rows = pl.ds(pl.multiple_of(z * ROWS, 8), ROWS)
        return jnp.concatenate([ref[0, rows, :], ref[1, rows, :]], axis=1)

    ones = jnp.ones((8, PLANE), F32)

    def hidden(t, z, v):
        v_hi = v.astype(BF16).astype(F32)
        v_low = v - v_hi
        x = jnp.concatenate([v_hi, v_low, v_hi, ones], axis=0).astype(BF16)
        xs[t, :, cells_of(z)] = x
        for c in range(2):
            rows = slice(256 * c, 256 * c + 256)
            act = jnp.dot(w_stack[rows, :], x, preferred_element_type=F32)
            hid[t, rows, cells_of(z)] = jnp.tanh(act).astype(BF16)

    def forward(t, z):
        if t == 0:
            v = loaded(start, z)
        else:
            pad = pads.at[t]
            v = select(wall_of(z), opposite(pad[z + 3]), streamed(pad, z, 1))
        hidden(t, z, v)
        if t < 2:
            change = jnp.dot(wo_trans[...], hid[t, :, cells_of(z)], preferred_element_type=F32)
            pads[t + 1, z + 3] = v + change + bias[...]

    def outgoing(z, g, slot):
        wall = wall_of(z)
        nothing = jnp.zeros((ROWS, PLANE), F32)
        bounce[z] = select(wall, opposite(g), nothing)
        pads[slot, z + 3] = select(wall, nothing, g)

    def backward(t, z):
        slot = (4, 3, 0)[t]
        g_post = streamed(pads.at[slot], z, -1) + bounce[z]
        acc_b[...] += g_post
        gb = jnp.concatenate([g_post, jnp.zeros((8, PLANE), F32)], axis=0).astype(BF16)
        gbs[:, cells_of(z)] = gb
        for c in range(2):
            rows = slice(256 * c, 256 * c + 256)
            dh = jnp.dot(wo[rows, :], gb, preferred_element_type=F32)
            h = hid[t, rows, cells_of(z)].astype(F32)
            dact[rows, cells_of(z)] = (dh * (1.0 - h * h)).astype(BF16)
        state[z] = g_post + jnp.dot(w_trans[...], dact[:, cells_of(z)], preferred_element_type=F32)

    def grads(t):
        g_in = lax.dot_general(dact[...], xs[t], NT, preferred_element_type=F32)
        g_out = lax.dot_general(hid[t], gbs[...], NT, preferred_element_type=F32)
        if t == 2:
            acc_in[...] = g_in
            acc_out[...] = g_out
        else:
            acc_in[...] += g_in
            acc_out[...] += g_out

    def halo(slot, sign):
        first, second = (up, down) if sign == 1 else (down, up)
        pad = pads.at[slot]
        if sign == 1:
            moves = [
                (pad.at[10, 0:16], pad.at[2, 0:16], up),
                (pad.at[8:10, 0:8], pad.at[0:2, 0:8], up),
                (pad.at[3, 8:24], pad.at[11, 8:24], down),
                (pad.at[4:6, 16:24], pad.at[12:14, 16:24], down),
            ]
        else:
            moves = [
                (pad.at[3, 0:16], pad.at[11, 0:16], down),
                (pad.at[4:6, 0:8], pad.at[12:14, 0:8], down),
                (pad.at[10, 8:24], pad.at[2, 8:24], up),
                (pad.at[8:10, 16:24], pad.at[0:2, 16:24], up),
            ]
        return [
            pltpu.make_async_remote_copy(
                src_ref=src, dst_ref=dst, send_sem=halo_send.at[slot, i], recv_sem=halo_recv.at[slot, i],
                device_id=to, device_id_type=MESH,
            )
            for i, (src, dst, to) in enumerate(moves)
        ]

    def begin(copies):
        for copy in copies:
            copy.start()

    def end(copies):
        for copy in copies:
            copy.wait_recv()

    def every(body):
        def two(i, carry):
            body(i)
            body(i + 4)
            return carry
        lax.fori_loop(0, 4, two, 0)

    def middle(body):
        body(3)
        body(4)

    def outer(body):
        def two(i, carry):
            body(i)
            body(i + 5)
            return carry
        lax.fori_loop(0, 3, two, 0)

    every(lambda z: forward(0, z))
    pl.semaphore_wait(barrier, len(peers))
    copy_1 = halo(1, 1)
    begin(copy_1)
    every(lambda z: outgoing(z, loaded(back_in, z), 0))
    copy_0 = halo(0, -1)
    begin(copy_0)
    middle(lambda z: forward(1, z))
    end(copy_1)
    outer(lambda z: forward(1, z))
    copy_2 = halo(2, 1)
    begin(copy_2)
    middle(lambda z: forward(2, z))
    end(copy_2)
    outer(lambda z: forward(2, z))
    end(copy_0)
    every(lambda z: backward(2, z))
    every(lambda z: outgoing(z, state[z], 3))
    copy_3 = halo(3, -1)
    begin(copy_3)
    grads(2)
    middle(lambda z: backward(1, z))
    end(copy_3)
    outer(lambda z: backward(1, z))
    every(lambda z: outgoing(z, state[z], 4))
    copy_4 = halo(4, -1)
    begin(copy_4)
    grads(1)
    middle(lambda z: backward(0, z))
    end(copy_4)
    outer(lambda z: backward(0, z))
    grads(0)

    exact = lax.Precision.HIGHEST
    upper = lax.dot_general(floats[64:88, :], acc_in[...], NT, precision=exact, preferred_element_type=F32)
    lower = lax.dot_general(floats[136:176, 0:48], acc_out[...], NT, precision=exact, preferred_element_type=F32)
    by_q = jnp.dot(floats[136:184, 0:ROWS], acc_b[...], precision=exact, preferred_element_type=F32)
    ordered = jnp.concatenate([by_q, jnp.zeros((80, PLANE), F32)], axis=0)
    line = lax.dot_general(jnp.ones((8, PLANE), F32), ordered, NT, precision=exact, preferred_element_type=F32)
    line = jnp.concatenate([line, jnp.zeros((8, HID - 128), F32)], axis=1)
    block = jnp.concatenate([upper, lower], axis=0)
    tail = jnp.where(lax.broadcasted_iota(jnp.int32, (8, HID), 0) == 7, line, block[56:64])
    block = jnp.concatenate([block[:56], tail], axis=0)
    for i in range(8):
        for j in range(4):
            parts[4 * i + j] = block[8 * i : 8 * i + 8, 128 * j : 128 * j + 128]

    def remote(src, dst, send, recv, to):
        return pltpu.make_async_remote_copy(
            src_ref=src, dst_ref=dst, send_sem=send, recv_sem=recv, device_id=to, device_id_type=MESH
        )

    mine = pl.multiple_of(core * 16, 16)
    other = pl.multiple_of((1 - core) * 16, 16)
    swap = remote(parts.at[pl.ds(other, 16)], from_core, core_send.at[0], core_recv.at[0], partner)
    swap.start()

    for half in range(2):
        for z in range(CZ):
            start[half, ROWS * z : ROWS * z + ROWS, :] = state[z, :, 128 * half : 128 * half + 128]
    for half in range(2):
        for row in range(Q):
            d_field[0, WHERE[row], :, 128 * half : 128 * half + 128] = start[half, pl.ds(row, CZ, stride=ROWS), :]

    swap.wait_recv()
    merged[...] = parts[pl.ds(mine, 16)] + from_core[...]
    per = 16 // ny
    scatter = []
    for k in range(ny - 1, 0, -1):
        piece = lax.rem(me_y + k, ny) * per
        scatter.append(remote(merged.at[pl.ds(piece, per)], from_y.at[k - 1], y_send.at[k - 1], y_recv.at[k - 1], at_y(k)))
    begin(scatter)
    end(scatter)
    total = merged[pl.ds(me_y * per, per)]
    for k in range(ny - 1):
        total = total + from_y[k]

    from_x[me_x] = total
    across = [
        remote(from_x.at[me_x], from_x.at[me_x], x_send.at[k - 1], x_recv.at[k - 1], at_x(k)) for k in range(1, nx)
    ]
    begin(across)
    end(across)
    total = from_x[0]
    for k in range(1, nx):
        total = total + from_x[k]

    from_z[me_z] = total
    far_first = sorted(range(1, nz), key=lambda k: -min(k, nz - k))
    along = [
        remote(from_z.at[me_z], from_z.at[me_z], z_send.at[k - 1], z_recv.at[k - 1], at_z(k)) for k in far_first
    ]
    begin(along)
    end(along)
    total = from_z[0]
    for k in range(1, nz):
        total = total + from_z[k]

    own = pl.ds(core * 16 + me_y * per, per)
    final[own] = total * scale
    spread_out = [
        remote(final.at[own], final.at[own], e_send.at[k - 1], e_recv.at[k - 1], at_y(k)) for k in range(ny - 1, 0, -1)
    ]
    begin(spread_out)
    end(spread_out)
    give = remote(final.at[pl.ds(mine, 16)], final.at[pl.ds(mine, 16)], core_send.at[1], core_recv.at[1], partner)
    give.start()
    give.wait_recv()
    for i in range(8):
        for j in range(4):
            sums[8 * i : 8 * i + 8, 128 * j : 128 * j + 128] = final[4 * i + j]

    for copies in (copy_0, copy_1, copy_2, copy_3, copy_4, [swap], scatter, across, along, spread_out, [give]):
        for copy in copies:
            copy.wait_send()


def solution(mesh):
    n_space, nx = mesh.shape["space"], mesh.shape["traj"]
    ny = 8 if n_space % 16 == 0 else 2
    nz = n_space // (2 * ny)
    scale = 1.0 / math.sqrt(float(n_space * nx * CELLS * STEPS))
    per = 16 // ny
    vmem = pl.BlockSpec(memory_space=pltpu.VMEM)
    dma = pltpu.SemaphoreType.DMA

    def per_device(field, solid, cotangent, w_in, b_in, w_out, b_out):
        def body(*refs):
            kernel((ny, nz, nx), scale, *refs)

        d_field, sums = pl.pallas_call(
            body,
            out_shape=(jax.ShapeDtypeStruct(field.shape, F32), jax.ShapeDtypeStruct((64, HID), F32)),
            in_specs=[vmem] * 9,
            out_specs=(vmem, vmem),
            scratch_shapes=[
                pltpu.VMEM((5, CZ + 6, ROWS, PLANE), F32),
                pltpu.VMEM((2, CZ * ROWS, 128), F32),
                pltpu.VMEM((2, CZ * ROWS, 128), F32),
                pltpu.VMEM((CZ, ROWS, PLANE), F32),
                pltpu.VMEM((CZ, ROWS, PLANE), F32),
                pltpu.VMEM((CZ, 8, PLANE), jnp.int32),
                pltpu.VMEM((STEPS, 128, CELLS), BF16),
                pltpu.VMEM((STEPS, HID, CELLS), BF16),
                pltpu.VMEM((HID, CELLS), BF16),
                pltpu.VMEM((48, CELLS), BF16),
                pltpu.VMEM((HID, 128), BF16),
                pltpu.VMEM((ROWS, HID), BF16),
                pltpu.VMEM((HID, 48), BF16),
                pltpu.VMEM((ROWS, HID), BF16),
                pltpu.VMEM((ROWS, PLANE), F32),
                pltpu.VMEM((HID, 128), F32),
                pltpu.VMEM((HID, 48), F32),
                pltpu.VMEM((ROWS, PLANE), F32),
                pltpu.VMEM((32, 8, 128), F32),
                pltpu.VMEM((16, 8, 128), F32),
                pltpu.VMEM((ny - 1, per, 8, 128), F32),
                pltpu.VMEM((nx, per, 8, 128), F32),
                pltpu.VMEM((nz, per, 8, 128), F32),
                pltpu.VMEM((16, 8, 128), F32),
                pltpu.VMEM((32, 8, 128), F32),
                dma((5, 4)), dma((5, 4)), dma((2,)), dma((2,)), dma((ny - 1,)), dma((ny - 1,)),
                dma((max(nx - 1, 1),)), dma((max(nx - 1, 1),)), dma((nz - 1,)), dma((nz - 1,)), dma((ny - 1,)), dma((ny - 1,)),
            ],
            compiler_params=pltpu.CompilerParams(collective_id=0, has_side_effects=True, vmem_limit_bytes=48 << 20),
            name="adjoint",
        )(field, solid, cotangent, w_in, b_in.reshape(1, HID), w_out.T, b_out.reshape(1, Q), jnp.asarray(FLOATS), jnp.asarray(INTS))
        return d_field, sums[:MOM], sums[MOM], sums[24:63].T, sums[63, :Q]

    return jax.shard_map(
        per_device,
        mesh=mesh,
        in_specs=(P("traj", None, "space", None), P("traj", "space", None), P("traj", None, "space", None), P(), P(), P(), P()),
        out_specs=(P("traj", None, "space", None), P(), P(), P(), P()),
        check_vma=False,
    )
```

time: 730 us -> 77.1 us (0.11)
  waiting for transfers between devices: 349 us -> 0 us
  blocking collectives: 110 us -> 0 us
  local copies, waits for them, and re-layouts: 112 us -> 9.7 us
  Pallas kernels: 0 us -> 66.3 us
  starting transfers between devices: 55.9 us -> 0 us
  matrix products: 47.5 us -> 0 us
  other arithmetic: 31.2 us -> 0 us
  between operations: 20.8 us -> 0.67 us
    psum x1 -> x0, waiting for transfers between devices: 341 us -> none  [per_device(): lax.psum((totals[0], totals[1], totals[2], totals[3]), ('space', 'traj'))]
    psum x1 -> x0, blocking collectives: 110 us -> none  [per_device(): lax.psum((totals[0], totals[1], totals[2], totals[3]), ('space', 'traj'))]
    dynamic_update_slice x80 -> x0, local copies, waits for them, and re-layouts: 72.8 us -> none  [collide_layers(): lax.map(lambda layer: collide_block(layer, weights, hermite)[0], layers)]
    pallas_call x0 -> x1, Pallas kernels: none -> 66.3 us  [per_device(): pl.pallas_call(body, out_shape=(jax.ShapeDtypeStruct(field.shape, F32), j...]
    ppermute x10 -> x0, starting transfers between devices: 55.8 us -> none  [the longest x5 42.5 us: padded_2(): after = lax.ppermute(first, axis, down)]
    dot_general x200 -> x0, matrix products: 47.5 us -> none  [the longest x40 9.95 us: collide_block(): jnp.dot(hermite, block, precision=lax.Precision.HIGHEST, preferred_elemen...]
    another operation x325 -> x0, local copies, waits for them, and re-layouts: 26.2 us -> none  [the longest x160 14 us: stream_local(): return jnp.stack(moved)]
    concatenate x220 -> x0, other arithmetic: 16.6 us -> none  [roll_plane(): return jnp.roll(grid, (along_x, along_y), (1, 2)).reshape(depth, NX * NY)]
  transfers between devices with their start and end apart: 11 -> 0, of which waited for: 5 -> 0; matrix products, arithmetic and copies ran while one was open for 1% -> 0% of each run, Pallas kernels for 0% -> 0%
where the time goes in v1:
time: 77.1 us; the launch traced here: 76.7 us
  Pallas kernels  66.3 us (86%)
  local copies, waits for them, and re-layouts  9.7 us (13%)
    pallas_call x1, Pallas kernels, per_device(): pl.pallas_call(body, out_shape=(jax.ShapeDtypeStruct(field.shape, F32), j...  66.3 us
    unnamed x19, local copies, waits for them, and re-layouts  7.34 us

profile of v1, /device:TPU:1, one launch (start us, length us, event | category | flops | bytes accessed | tf_op | source)
XLA Modules:
  0.0 76.7 jit_solution(11002041202787608125)
XLA Ops:
  0.6 0.0 copy-start.7
  0.6 0.0 copy-start.8
  0.7 0.7 copy-done.7
  1.3 0.0 copy-done.8
  1.3 0.0 copy-start
  1.3 1.0 %copy-done = f32[1,39,8,256]{3,2,1,0:T(8,128)S(1)} copy-done((f32[1,39,8,256]{3,2,1,0:T(8,128)S(1)}, f32[1,39,8,256]{3,2,1,0:T(8,128)}, u32[]{:S(2)}) %copy-start) | copy-done | bytes 319512
  2.3 0.0 copy-start.1
  2.3 1.0 %copy-done.1 = f32[1,39,8,256]{3,2,1,0:T(8,128)S(1)} copy-done((f32[1,39,8,256]{3,2,1,0:T(8,128)S(1)}, f32[1,39,8,256]{3,2,1,0:T(8,128)}, u32[]{:S(2)}) %copy-start.1) | copy-done | bytes 319512
  3.3 0.0 copy-start.2
  3.3 0.9 %copy-done.2 = f32[320,128]{1,0:T(8,128)S(1)} copy-done((f32[320,128]{1,0:T(8,128)S(1)}, f32[320,128]{1,0:T(8,128)}, u32[]{:S(2)}) %copy-start.2) | copy-done | bytes 163864
  4.2 0.0 copy-start.3
  4.2 0.9 %copy-done.3 = s32[4,40,128]{2,1,0:T(8,128)S(1)} copy-done((s32[4,40,128]{2,1,0:T(8,128)S(1)}, s32[4,40,128]{2,1,0:T(8,128)}, u32[]{:S(2)}) %copy-start.3) | copy-done | bytes 81944
  5.1 0.0 copy-start.4
  5.1 0.8 %copy-done.4 = bf16[512,39]{0,1:T(8,128)(2,1)S(1)} copy-done((bf16[512,39]{0,1:T(8,128)(2,1)S(1)}, bf16[512,39]{0,1:T(8,128)(2,1)}, u32[]{:S(2)}) %copy-start.4) | copy-done | bytes 39960
  5.8 0.0 copy-start.5
  5.8 0.7 copy-done.5
  6.6 0.0 copy-start.6
  6.6 0.7 copy-done.6
  7.3 66.3 %adjoint.1 = (f32[1,39,8,256]{3,2,1,0:T(8,128)S(1)}, f32[64,512]{1,0:T(8,128)S(1)}) custom-call(f32[1,39,8,256]{3,2,1,0:T(8,128)S(1)} %copy-done, s32[1,8,256]{2,1,0:T(8,128)S(1)} %copy-done.6, f32[1,39,8,256]{3,2,1,0:T(8,128)S(1)} %copy-done.1, bf16[20,512]{1,0:T(8,128)(2,1)S(1)} %copy-done.5, f32[1,512]{1,0:T(1,128)S(1)} %bitcast.9, ...), custom_call_target="tpu_custom_call" | custom-call | tf_op jit(solution)/shard_map/adjoint/pallas_call | solution.py:466
  73.6 0.5 slice_bitcast_fusion.1
  74.1 0.6 slice.13
  74.7 0.6 slice.12
  75.3 0.6 slice_bitcast_fusion
  75.9 0.7 copy.15
Async XLA Ops:
  0.6 0.7 copy-start.7
  0.6 0.7 copy-start.8
  1.3 1.0 %copy-start = (f32[1,39,8,256]{3,2,1,0:T(8,128)S(1)}, f32[1,39,8,256]{3,2,1,0:T(8,128)}, u32[]{:S(2)}) copy-start(f32[1,39,8,256]{3,2,1,0:T(8,128)} %refs_0_.1) | copy-start | bytes 958468
  2.3 1.0 %copy-start.1 = (f32[1,39,8,256]{3,2,1,0:T(8,128)S(1)}, f32[1,39,8,256]{3,2,1,0:T(8,128)}, u32[]{:S(2)}) copy-start(f32[1,39,8,256]{3,2,1,0:T(8,128)} %refs_2_.1) | copy-start | bytes 958468
  3.3 0.9 %copy-start.2 = (f32[320,128]{1,0:T(8,128)S(1)}, f32[320,128]{1,0:T(8,128)}, u32[]{:S(2)}) copy-start(f32[320,128]{1,0:T(8,128)} %constant.4.clone.refs_7_) | copy-start | bytes 491524
  4.2 0.9 %copy-start.3 = (s32[4,40,128]{2,1,0:T(8,128)S(1)}, s32[4,40,128]{2,1,0:T(8,128)}, u32[]{:S(2)}) copy-start(s32[4,40,128]{2,1,0:T(8,128)} %constant.5.clone.refs_8_) | copy-start | bytes 245764
  5.1 0.8 %copy-start.4 = (bf16[512,39]{0,1:T(8,128)(2,1)S(1)}, bf16[512,39]{0,1:T(8,128)(2,1)}, u32[]{:S(2)}) copy-start(bf16[512,39]{0,1:T(8,128)(2,1)} %param.14) | copy-start | bytes 119812
  5.8 0.7 copy-start.5
  6.6 0.7 copy-start.6

commit v2 on v1

--- a/solution.py
+++ b/solution.py
@@ -112,7 +112,9 @@
     floats[88:136] = pick
     floats[136:184, :48] = pick.T[:48, :48]
     floats[184:224, :64] = thick.T
-    ints = np.zeros((4, ROWS, 128), np.int32)
+    ints = np.zeros((5, ROWS, 128), np.int32)
+    for row, q in enumerate(where):
+        ints[4, :, q] = row
     for row, e in enumerate(order):
         for back, sign in ((0, 1), (1, -1)):
             for lane in range(128):
@@ -121,6 +123,7 @@
                 ints[2 * back, row, lane] = source % 128
                 ints[2 * back + 1, row, lane] = source // 128
     ints[0, 39], ints[2, 39] = np.arange(128), np.arange(128)
+    ints[4, :, Q:] = ROWS - 1
     return where, floats, ints
 
 
@@ -128,11 +131,14 @@
 
 
 def kernel(
-    grid, scale, field, solid, cotangent, w_in, b_in, w_out, b_out, floats, ints, d_field, sums,
-    pads, start, back_in, state, bounce, walls, xs, hid, dact, gbs, w_stack, w_trans, wo, wo_trans, bias, acc_in, acc_out,
+    grid, scale, *refs
+):
+    (
+    field_at, solid_at, cotangent_at, w_in_at, b_in_at, w_out_at, b_out_at, floats_at, ints_at, d_field, sums,
+    field, solid, cotangent, w_in, b_in, w_out, b_out, floats, ints, by_q, in_sem, out_sem, pads, start, back_in, state, bounce, walls, xs, hid, dact, gbs, w_stack, w_trans, wo, wo_trans, bias, acc_in, acc_out,
     acc_b, parts, from_core, from_y, from_x, from_z, merged, final,
     halo_send, halo_recv, core_send, core_recv, y_send, y_recv, x_send, x_recv, z_send, z_recv, e_send, e_recv,
-):
+    ) = refs
     ny, nz, nx = grid
     me_s, me_x = lax.axis_index("space"), lax.axis_index("traj")
     core = lax.rem(me_s, 2)
@@ -151,6 +157,20 @@
     barrier = pltpu.get_barrier_semaphore()
     for peer in peers:
         pl.semaphore_signal(barrier, inc=1, device_id=peer, device_id_type=MESH)
+
+    copies_in = [
+        pltpu.make_async_copy(src, dst, in_sem.at[i])
+        for i, (src, dst) in enumerate(
+            [
+                (floats_at, floats), (w_in_at, w_in), (b_in_at, b_in), (w_out_at, w_out), (b_out_at, b_out),
+                (field_at, field), (solid_at, solid), (ints_at, ints), (cotangent_at, cotangent),
+            ]
+        )
+    ]
+    for copy in copies_in:
+        copy.start()
+    for copy in copies_in[:5]:
+        copy.wait()
 
     w = w_in[...].astype(F32)
     b = b_in[...]
@@ -176,17 +196,16 @@
     acc_b[...] = jnp.zeros((ROWS, PLANE), F32)
 
     zeros = jnp.zeros((CZ, 128), F32)
-    for half in range(2):
-        lanes = slice(128 * half, 128 * half + 128)
-        for row in range(ROWS):
-            if row < Q:
-                start[half, pl.ds(row, CZ, stride=ROWS), :] = field[0, WHERE[row], :, lanes]
-                back_in[half, pl.ds(row, CZ, stride=ROWS), :] = cotangent[0, WHERE[row], :, lanes]
-            else:
-                start[half, pl.ds(row, CZ, stride=ROWS), :] = zeros
-                back_in[half, pl.ds(row, CZ, stride=ROWS), :] = zeros
-    for z in range(CZ):
-        walls[z] = jnp.broadcast_to(solid[0, z : z + 1, :], (8, PLANE))
+
+    def by_plane(source, rows):
+        for half in range(2):
+            lanes = slice(128 * half, 128 * half + 128)
+            for row in range(ROWS):
+                value = source[0, WHERE[row], :, lanes] if row < Q else zeros
+                rows[half, pl.ds(row, CZ, stride=ROWS), :] = value
+
+    copies_in[5].wait()
+    by_plane(field, start)
 
     row8 = lax.broadcasted_iota(jnp.int32, (8, PLANE), 0)
 
@@ -224,34 +243,47 @@
         return jnp.concatenate([jnp.where(far, right, left), jnp.where(far, left, right)], axis=1)
 
     def cells_of(z):
-        return pl.ds(pl.multiple_of(z * PLANE, PLANE), PLANE)
+        return slice(z * PLANE, z * PLANE + PLANE)
 
     def loaded(ref, z):
-        rows = pl.ds(pl.multiple_of(z * ROWS, 8), ROWS)
+        rows = slice(z * ROWS, z * ROWS + ROWS)
         return jnp.concatenate([ref[0, rows, :], ref[1, rows, :]], axis=1)
 
-    ones = jnp.ones((8, PLANE), F32)
-
-    def hidden(t, z, v):
+    ones = jnp.ones((8, 2 * PLANE), F32)
+
+    def side_by_side(parts):
+        return jnp.concatenate(parts, axis=1)
+
+    def forward_hidden(t, pair):
+        values = []
+        for z in pair:
+            if t == 0:
+                values.append(loaded(start, z))
+            else:
+                pad = pads.at[t]
+                values.append(select(wall_of(z), opposite(pad[z + 3]), streamed(pad, z, 1)))
+        v = side_by_side(values)
         v_hi = v.astype(BF16).astype(F32)
-        v_low = v - v_hi
-        x = jnp.concatenate([v_hi, v_low, v_hi, ones], axis=0).astype(BF16)
-        xs[t, :, cells_of(z)] = x
+        x = jnp.concatenate([v_hi, v - v_hi, v_hi, ones], axis=0).astype(BF16)
+        for i, z in enumerate(pair):
+            xs[t, :, cells_of(z)] = x[:, PLANE * i : PLANE * i + PLANE]
+        halves = []
         for c in range(2):
             rows = slice(256 * c, 256 * c + 256)
             act = jnp.dot(w_stack[rows, :], x, preferred_element_type=F32)
-            hid[t, rows, cells_of(z)] = jnp.tanh(act).astype(BF16)
-
-    def forward(t, z):
-        if t == 0:
-            v = loaded(start, z)
-        else:
-            pad = pads.at[t]
-            v = select(wall_of(z), opposite(pad[z + 3]), streamed(pad, z, 1))
-        hidden(t, z, v)
+            h = jnp.tanh(act).astype(BF16)
+            for i, z in enumerate(pair):
+                hid[t, rows, cells_of(z)] = h[:, PLANE * i : PLANE * i + PLANE]
+            halves.append(h)
+        return v, jnp.concatenate(halves, axis=0)
+
+    def forward_change(t, pair, done):
         if t < 2:
-            change = jnp.dot(wo_trans[...], hid[t, :, cells_of(z)], preferred_element_type=F32)
-            pads[t + 1, z + 3] = v + change + bias[...]
+            v, h = done
+            change = jnp.dot(wo_trans[...], h, preferred_element_type=F32)
+            for i, z in enumerate(pair):
+                cut = slice(PLANE * i, PLANE * i + PLANE)
+                pads[t + 1, z + 3] = v[:, cut] + change[:, cut] + bias[...]
 
     def outgoing(z, g, slot):
         wall = wall_of(z)
@@ -259,22 +291,38 @@
         bounce[z] = select(wall, opposite(g), nothing)
         pads[slot, z + 3] = select(wall, nothing, g)
 
-    def backward(t, z):
+    def backward_hidden(t, pair):
         slot = (4, 3, 0)[t]
-        g_post = streamed(pads.at[slot], z, -1) + bounce[z]
-        acc_b[...] += g_post
-        gb = jnp.concatenate([g_post, jnp.zeros((8, PLANE), F32)], axis=0).astype(BF16)
-        gbs[:, cells_of(z)] = gb
+        posts = [streamed(pads.at[slot], z, -1) + bounce[z] for z in pair]
+        acc_b[...] += posts[0] + posts[1]
+        g_post = side_by_side(posts)
+        gb = jnp.concatenate([g_post, jnp.zeros((8, 2 * PLANE), F32)], axis=0).astype(BF16)
+        for i, z in enumerate(pair):
+            gbs[:, cells_of(z)] = gb[:, PLANE * i : PLANE * i + PLANE]
+        halves = []
         for c in range(2):
             rows = slice(256 * c, 256 * c + 256)
             dh = jnp.dot(wo[rows, :], gb, preferred_element_type=F32)
-            h = hid[t, rows, cells_of(z)].astype(F32)
-            dact[rows, cells_of(z)] = (dh * (1.0 - h * h)).astype(BF16)
-        state[z] = g_post + jnp.dot(w_trans[...], dact[:, cells_of(z)], preferred_element_type=F32)
+            h = side_by_side([hid[t, rows, cells_of(z)] for z in pair]).astype(F32)
+            da = (dh * (1.0 - h * h)).astype(BF16)
+            for i, z in enumerate(pair):
+                dact[rows, cells_of(z)] = da[:, PLANE * i : PLANE * i + PLANE]
+            halves.append(da)
+        return g_post, jnp.concatenate(halves, axis=0)
+
+    def backward_change(t, pair, done):
+        g_post, da = done
+        g = g_post + jnp.dot(w_trans[...], da, preferred_element_type=F32)
+        for i, z in enumerate(pair):
+            cut = slice(PLANE * i, PLANE * i + PLANE)
+            if t > 0:
+                outgoing(z, g[:, cut], 5 - t)
+            else:
+                state[z] = g[:, cut]
 
     def grads(t):
-        g_in = lax.dot_general(dact[...], xs[t], NT, preferred_element_type=F32)
-        g_out = lax.dot_general(hid[t], gbs[...], NT, preferred_element_type=F32)
+        g_in = lax.dot_general(xs[t], dact[...], NT, preferred_element_type=F32)
+        g_out = lax.dot_general(gbs[...], hid[t], NT, preferred_element_type=F32)
         if t == 2:
             acc_in[...] = g_in
             acc_out[...] = g_out
@@ -315,70 +363,79 @@
         for copy in copies:
             copy.wait_recv()
 
-    def every(body):
-        def two(i, carry):
-            body(i)
-            body(i + 4)
-            return carry
-        lax.fori_loop(0, 4, two, 0)
-
-    def middle(body):
-        body(3)
-        body(4)
-
-    def outer(body):
-        def two(i, carry):
-            body(i)
-            body(i + 5)
-            return carry
-        lax.fori_loop(0, 3, two, 0)
-
-    every(lambda z: forward(0, z))
+    MIDDLE, OUTER = [(3, 4)], [(0, 1), (2, 5), (6, 7)]
+
+    def in_turn(first, second, t, pairs, before=None):
+        done = None
+        for pair in pairs:
+            if before is not None and pair in OUTER:
+                end(before)
+                before = None
+            now = first(t, pair)
+            if done is not None:
+                second(t, *done)
+            done = (pair, now)
+        second(t, *done)
+
+    def forwards(t, before=None):
+        in_turn(forward_hidden, forward_change, t, MIDDLE + OUTER, before)
+
+    def backwards(t, before=None):
+        in_turn(backward_hidden, backward_change, t, MIDDLE + OUTER, before)
+
+    forwards(0)
+    for copy in copies_in[6:8]:
+        copy.wait()
     pl.semaphore_wait(barrier, len(peers))
     copy_1 = halo(1, 1)
     begin(copy_1)
-    every(lambda z: outgoing(z, loaded(back_in, z), 0))
+    for z in range(CZ):
+        walls[z] = jnp.broadcast_to(solid[0, z : z + 1, :], (8, PLANE))
+    copies_in[8].wait()
+    by_plane(cotangent, back_in)
+    for z in range(CZ):
+        outgoing(z, loaded(back_in, z), 0)
     copy_0 = halo(0, -1)
     begin(copy_0)
-    middle(lambda z: forward(1, z))
-    end(copy_1)
-    outer(lambda z: forward(1, z))
+    forwards(1, copy_1)
     copy_2 = halo(2, 1)
     begin(copy_2)
-    middle(lambda z: forward(2, z))
-    end(copy_2)
-    outer(lambda z: forward(2, z))
-    end(copy_0)
-    every(lambda z: backward(2, z))
-    every(lambda z: outgoing(z, state[z], 3))
+    forwards(2, copy_2)
+    backwards(2, copy_0)
     copy_3 = halo(3, -1)
     begin(copy_3)
     grads(2)
-    middle(lambda z: backward(1, z))
-    end(copy_3)
-    outer(lambda z: backward(1, z))
-    every(lambda z: outgoing(z, state[z], 4))
+    backwards(1, copy_3)
     copy_4 = halo(4, -1)
     begin(copy_4)
     grads(1)
-    middle(lambda z: backward(0, z))
-    end(copy_4)
-    outer(lambda z: backward(0, z))
+    backwards(0, copy_4)
     grads(0)
 
-    exact = lax.Precision.HIGHEST
-    upper = lax.dot_general(floats[64:88, :], acc_in[...], NT, precision=exact, preferred_element_type=F32)
-    lower = lax.dot_general(floats[136:176, 0:48], acc_out[...], NT, precision=exact, preferred_element_type=F32)
-    by_q = jnp.dot(floats[136:184, 0:ROWS], acc_b[...], precision=exact, preferred_element_type=F32)
-    ordered = jnp.concatenate([by_q, jnp.zeros((80, PLANE), F32)], axis=0)
-    line = lax.dot_general(jnp.ones((8, PLANE), F32), ordered, NT, precision=exact, preferred_element_type=F32)
-    line = jnp.concatenate([line, jnp.zeros((8, HID - 128), F32)], axis=1)
-    block = jnp.concatenate([upper, lower], axis=0)
-    tail = jnp.where(lax.broadcasted_iota(jnp.int32, (8, HID), 0) == 7, line, block[56:64])
-    block = jnp.concatenate([block[:56], tail], axis=0)
-    for i in range(8):
+    def two(v):
+        v_hi = v.astype(BF16).astype(F32)
+        return v_hi, v - v_hi
+
+    a_hi, a_low = two(acc_in[...])
+    f_hi, f_low = two(floats[64:88, :])
+    left = jnp.concatenate([f_hi, f_hi], axis=1).astype(BF16)
+    right = jnp.concatenate([a_hi, a_low], axis=0).astype(BF16)
+    upper = jnp.dot(left, right, preferred_element_type=F32)
+    upper = upper + jnp.dot(f_low.astype(BF16), a_hi.astype(BF16), preferred_element_type=F32)
+    b_hi, b_low = two(acc_b[...])
+    pair = jnp.concatenate([b_hi, jnp.zeros((24, PLANE), F32), b_low, jnp.zeros((24, PLANE), F32)], axis=0).astype(BF16)
+    line = lax.dot_general(jnp.ones((8, PLANE), BF16), pair, NT, preferred_element_type=F32)
+    line = line + jnp.concatenate([line[:, 64:], line[:, :64]], axis=1)
+    line = jnp.take_along_axis(line, ints[4, 0:8], axis=1, mode="promise_in_bounds")
+    for i in range(3):
         for j in range(4):
-            parts[4 * i + j] = block[8 * i : 8 * i + 8, 128 * j : 128 * j + 128]
+            parts[4 * i + j] = upper[8 * i : 8 * i + 8, 128 * j : 128 * j + 128]
+    for row in range(Q):
+        i, k = divmod(WHERE[row] + 24, 8)
+        for j in range(4):
+            parts[4 * i + j, k : k + 1, :] = acc_out[row : row + 1, 128 * j : 128 * j + 128]
+    for j in range(4):
+        parts[28 + j, 7:8, :] = line[0:1] if j == 0 else jnp.zeros((1, 128), F32)
 
     def remote(src, dst, send, recv, to):
         return pltpu.make_async_remote_copy(
@@ -395,8 +452,10 @@
             start[half, ROWS * z : ROWS * z + ROWS, :] = state[z, :, 128 * half : 128 * half + 128]
     for half in range(2):
         for row in range(Q):
-            d_field[0, WHERE[row], :, 128 * half : 128 * half + 128] = start[half, pl.ds(row, CZ, stride=ROWS), :]
-
+            by_q[0, WHERE[row], :, 128 * half : 128 * half + 128] = start[half, pl.ds(row, CZ, stride=ROWS), :]
+
+    field_out = pltpu.make_async_copy(by_q, d_field, out_sem.at[0])
+    field_out.start()
     swap.wait_recv()
     merged[...] = parts[pl.ds(mine, 16)] + from_core[...]
     per = 16 // ny
@@ -441,13 +500,42 @@
     give = remote(final.at[pl.ds(mine, 16)], final.at[pl.ds(mine, 16)], core_send.at[1], core_recv.at[1], partner)
     give.start()
     give.wait_recv()
-    for i in range(8):
-        for j in range(4):
-            sums[8 * i : 8 * i + 8, 128 * j : 128 * j + 128] = final[4 * i + j]
-
+    sums_out = pltpu.make_async_copy(final, sums, out_sem.at[1])
+    sums_out.start()
     for copies in (copy_0, copy_1, copy_2, copy_3, copy_4, [swap], scatter, across, along, spread_out, [give]):
         for copy in copies:
             copy.wait_send()
+    field_out.wait()
+    sums_out.wait()
+
+
+def write_out(field_at, sums_at, d_field, g_w_in, g_b_in, g_w_out, g_b_out, field, sums, a, b, c, d, sem):
+    field_in = pltpu.make_async_copy(field_at, field, sem.at[0])
+    sums_in = pltpu.make_async_copy(sums_at, sums, sem.at[1])
+    sums_in.start()
+    field_in.start()
+    sums_in.wait()
+    for j in range(4):
+        cut = slice(128 * j, 128 * j + 128)
+        a[0:8, cut] = sums[j]
+        a[8:16, cut] = sums[4 + j]
+        a[16:20, cut] = sums[8 + j, 0:4]
+        b[:, cut] = sums[8 + j, 4:5]
+        for i in range(3, 7):
+            c[8 * i - 24 : 8 * i - 16, cut] = sums[4 * i + j]
+        c[32:39, cut] = sums[28 + j, 0:7]
+    d[...] = sums[28, 7:8, 0:Q]
+    small = [
+        pltpu.make_async_copy(src, dst, sem.at[i])
+        for i, (src, dst) in enumerate([(a, g_w_in), (b, g_b_in), (c, g_w_out), (d, g_b_out)], 2)
+    ]
+    for copy in small:
+        copy.start()
+    field_in.wait()
+    big = pltpu.make_async_copy(field, d_field, sem.at[6])
+    big.start()
+    for copy in small + [big]:
+        copy.wait()
 
 
 def solution(mesh):
@@ -456,7 +544,7 @@
     nz = n_space // (2 * ny)
     scale = 1.0 / math.sqrt(float(n_space * nx * CELLS * STEPS))
     per = 16 // ny
-    vmem = pl.BlockSpec(memory_space=pltpu.VMEM)
+    hbm = pl.BlockSpec(memory_space=pltpu.HBM)
     dma = pltpu.SemaphoreType.DMA
 
     def per_device(field, solid, cotangent, w_in, b_in, w_out, b_out):
@@ -465,10 +553,22 @@
 
         d_field, sums = pl.pallas_call(
             body,
-            out_shape=(jax.ShapeDtypeStruct(field.shape, F32), jax.ShapeDtypeStruct((64, HID), F32)),
-            in_specs=[vmem] * 9,
-            out_specs=(vmem, vmem),
+            out_shape=(jax.ShapeDtypeStruct(field.shape, F32), jax.ShapeDtypeStruct((32, 8, 128), F32)),
+            in_specs=[hbm] * 9,
+            out_specs=(hbm, hbm),
             scratch_shapes=[
+                pltpu.VMEM(field.shape, F32),
+                pltpu.VMEM(solid.shape, jnp.int32),
+                pltpu.VMEM(field.shape, F32),
+                pltpu.VMEM(w_in.shape, BF16),
+                pltpu.VMEM((1, HID), F32),
+                pltpu.VMEM((Q, HID), BF16),
+                pltpu.VMEM((1, Q), F32),
+                pltpu.VMEM(FLOATS.shape, F32),
+                pltpu.VMEM(INTS.shape, jnp.int32),
+                pltpu.VMEM(field.shape, F32),
+                dma((9,)),
+                dma((2,)),
                 pltpu.VMEM((5, CZ + 6, ROWS, PLANE), F32),
                 pltpu.VMEM((2, CZ * ROWS, 128), F32),
                 pltpu.VMEM((2, CZ * ROWS, 128), F32),
@@ -484,8 +584,8 @@
                 pltpu.VMEM((HID, 48), BF16),
                 pltpu.VMEM((ROWS, HID), BF16),
                 pltpu.VMEM((ROWS, PLANE), F32),
-                pltpu.VMEM((HID, 128), F32),
-                pltpu.VMEM((HID, 48), F32),
+                pltpu.VMEM((128, HID), F32),
+                pltpu.VMEM((48, HID), F32),
                 pltpu.VMEM((ROWS, PLANE), F32),
                 pltpu.VMEM((32, 8, 128), F32),
                 pltpu.VMEM((16, 8, 128), F32),
@@ -497,10 +597,29 @@
                 dma((5, 4)), dma((5, 4)), dma((2,)), dma((2,)), dma((ny - 1,)), dma((ny - 1,)),
                 dma((max(nx - 1, 1),)), dma((max(nx - 1, 1),)), dma((nz - 1,)), dma((nz - 1,)), dma((ny - 1,)), dma((ny - 1,)),
             ],
-            compiler_params=pltpu.CompilerParams(collective_id=0, has_side_effects=True, vmem_limit_bytes=48 << 20),
+            compiler_params=pltpu.CompilerParams(collective_id=0, has_side_effects=True, vmem_limit_bytes=62 << 20),
             name="adjoint",
         )(field, solid, cotangent, w_in, b_in.reshape(1, HID), w_out.T, b_out.reshape(1, Q), jnp.asarray(FLOATS), jnp.asarray(INTS))
-        return d_field, sums[:MOM], sums[MOM], sums[24:63].T, sums[63, :Q]
+        d_field, g_w_in, g_b_in, g_w_out, g_b_out = pl.pallas_call(
+            write_out,
+            out_shape=(
+                jax.ShapeDtypeStruct(field.shape, F32),
+                jax.ShapeDtypeStruct((MOM, HID), F32),
+                jax.ShapeDtypeStruct((1, HID), F32),
+                jax.ShapeDtypeStruct((Q, HID), F32),
+                jax.ShapeDtypeStruct((1, Q), F32),
+            ),
+            in_specs=[hbm, hbm],
+            out_specs=(hbm,) * 5,
+            scratch_shapes=[
+                pltpu.VMEM(field.shape, F32), pltpu.VMEM((32, 8, 128), F32),
+                pltpu.VMEM((MOM, HID), F32), pltpu.VMEM((1, HID), F32), pltpu.VMEM((Q, HID), F32), pltpu.VMEM((1, Q), F32),
+                dma((7,)),
+            ],
+            compiler_params=pltpu.CompilerParams(vmem_limit_bytes=62 << 20),
+            name="write_out",
+        )(d_field, sums)
+        return d_field, g_w_in, g_b_in.reshape(HID), g_w_out.T, g_b_out.reshape(Q)
 
     return jax.shard_map(
         per_device,

time: 77.1 us -> 63.4 us (0.82)
  local copies, waits for them, and re-layouts: 9.7 us -> 0 us
  Pallas kernels: 66.3 us -> 62.5 us
    unnamed x19 -> x0, local copies, waits for them, and re-layouts: 7.34 us -> none
    pallas_call x1, Pallas kernels: 66.3 us -> 60.7 us  [per_device(): pl.pallas_call(body, out_shape=(jax.ShapeDtypeStruct(field.shape, F32), j...]
    pallas_call x0 -> x1, Pallas kernels: none -> 1.82 us  [per_device(): pl.pallas_call(write_out, out_shape=(jax.ShapeDtypeStruct(field.shape, F3...]
    slice x2 -> x0, local copies, waits for them, and re-layouts: 1.2 us -> none  [per_device(): return (d_field, sums[:MOM], sums[MOM], sums[24:63].T, sums[63, :Q])]
where the time goes in v2:
time: 63.4 us; the launch traced here: 63.2 us
  Pallas kernels  62.5 us (99%)
  between operations  0.64 us (1%)
    pallas_call x1, Pallas kernels, per_device(): pl.pallas_call(body, out_shape=(jax.ShapeDtypeStruct(field.shape, F32), j...  60.7 us
    pallas_call x1, Pallas kernels, per_device(): pl.pallas_call(write_out, out_shape=(jax.ShapeDtypeStruct(field.shape, F3...  1.82 us

profile of v2, /device:TPU:1, one launch (start us, length us, event | category | flops | bytes accessed | tf_op | source)
XLA Modules:
  0.0 63.2 jit_solution(3582421564183488718)
XLA Ops:
  0.6 60.7 %adjoint.1 = (f32[1,39,8,256]{3,2,1,0:T(8,128)}, f32[32,8,128]{2,1,0:T(8,128)}) custom-call(f32[1,39,8,256]{3,2,1,0:T(8,128)} %refs_0_.1, s32[1,8,256]{2,1,0:T(8,128)} %refs_1_.1, f32[1,39,8,256]{3,2,1,0:T(8,128)} %refs_2_.1, bf16[20,512]{1,0:T(8,128)(2,1)} %refs_3_.1, f32[1,512]{1,0:T(1,128)} %bitcast.7, bf16[39,512]{1,0:T(8,128)(2,1)} %bitcast.6, ...), custom_call_target="tpu_custom_call" | custom-call | tf_op jit(solution)/shard_map/adjoint/pallas_call | solution.py:554
  61.4 1.8 %write_out.1 = (f32[1,39,8,256]{3,2,1,0:T(8,128)}, f32[20,512]{1,0:T(8,128)}, f32[1,512]{1,0:T(1,128)}, f32[39,512]{1,0:T(8,128)}, f32[1,39]{1,0:T(1,128)}) custom-call(f32[1,39,8,256]{3,2,1,0:T(8,128)} %get-tuple-element.12.field_at, f32[32,8,128]{2,1,0:T(8,128)} %get-tuple-element.13.sums_at), custom_call_target="tpu_custom_call" | custom-call | tf_op jit(solution)/shard_map/write_out/pallas_call | solution.py:603

commit v3 on v2

--- a/solution.py
+++ b/solution.py
@@ -135,9 +135,9 @@
 ):
     (
     field_at, solid_at, cotangent_at, w_in_at, b_in_at, w_out_at, b_out_at, floats_at, ints_at, d_field, sums,
-    field, solid, cotangent, w_in, b_in, w_out, b_out, floats, ints, by_q, in_sem, out_sem, pads, start, back_in, state, bounce, walls, xs, hid, dact, gbs, w_stack, w_trans, wo, wo_trans, bias, acc_in, acc_out,
+    field, solid, cotangent, w_in, b_in, w_out, b_out, floats, ints, by_q, in_sem, out_sem, pads, start, back_in, state, bounce, walls, xs, hid, dact, dhs, gbs, w_stack, w_trans, wo, wo_trans, bias, acc_in, acc_out,
     acc_b, parts, from_core, from_y, from_x, from_z, merged, final,
-    halo_send, halo_recv, core_send, core_recv, y_send, y_recv, x_send, x_recv, z_send, z_recv, e_send, e_recv,
+    halo_send, halo_recv, core_send, core_recv, y_send, y_recv, x_send, x_recv, z_send, z_recv, e_send, e_recv, g_send, g_recv,
     ) = refs
     ny, nz, nx = grid
     me_s, me_x = lax.axis_index("space"), lax.axis_index("traj")
@@ -271,14 +271,24 @@
         for c in range(2):
             rows = slice(256 * c, 256 * c + 256)
             act = jnp.dot(w_stack[rows, :], x, preferred_element_type=F32)
-            h = jnp.tanh(act).astype(BF16)
+            wide = jnp.tanh(act)
+            h = wide.astype(BF16)
             for i, z in enumerate(pair):
                 hid[t, rows, cells_of(z)] = h[:, PLANE * i : PLANE * i + PLANE]
+            if t == 2:
+                wide = h.astype(F32)
+                dh = side_by_side([dhs[rows, cells_of(z)] for z in pair]).astype(F32)
+                h = (dh * (1.0 - wide * wide)).astype(BF16)
+                for i, z in enumerate(pair):
+                    dact[rows, cells_of(z)] = h[:, PLANE * i : PLANE * i + PLANE]
             halves.append(h)
         return v, jnp.concatenate(halves, axis=0)
 
     def forward_change(t, pair, done):
-        if t < 2:
+        if t == 2:
+            g = side_by_side([state[z] for z in pair])
+            backward_change(2, pair, (g, done[1]))
+        else:
             v, h = done
             change = jnp.dot(wo_trans[...], h, preferred_element_type=F32)
             for i, z in enumerate(pair):
@@ -291,7 +301,7 @@
         bounce[z] = select(wall, opposite(g), nothing)
         pads[slot, z + 3] = select(wall, nothing, g)
 
-    def backward_hidden(t, pair):
+    def backward_post(t, pair):
         slot = (4, 3, 0)[t]
         posts = [streamed(pads.at[slot], z, -1) + bounce[z] for z in pair]
         acc_b[...] += posts[0] + posts[1]
@@ -299,6 +309,20 @@
         gb = jnp.concatenate([g_post, jnp.zeros((8, 2 * PLANE), F32)], axis=0).astype(BF16)
         for i, z in enumerate(pair):
             gbs[:, cells_of(z)] = gb[:, PLANE * i : PLANE * i + PLANE]
+            if t != 1:
+                state[z] = posts[i]
+        return g_post, gb
+
+    def backward_ahead(pair):
+        g_post, gb = backward_post(2, pair)
+        for c in range(2):
+            rows = slice(256 * c, 256 * c + 256)
+            dh = jnp.dot(wo[rows, :], gb, preferred_element_type=F32).astype(BF16)
+            for i, z in enumerate(pair):
+                dhs[rows, cells_of(z)] = dh[:, PLANE * i : PLANE * i + PLANE]
+
+    def backward_hidden(t, pair):
+        g_post, gb = backward_post(t, pair)
         halves = []
         for c in range(2):
             rows = slice(256 * c, 256 * c + 256)
@@ -310,15 +334,20 @@
             halves.append(da)
         return g_post, jnp.concatenate(halves, axis=0)
 
+    def backward_field(pair):
+        da = side_by_side([dact[:, cells_of(z)] for z in pair])
+        change = jnp.dot(w_trans[...], da, preferred_element_type=F32)
+        for i, z in enumerate(pair):
+            g = state[z] + change[:, PLANE * i : PLANE * i + PLANE]
+            for half in range(2):
+                start[half, ROWS * z : ROWS * z + ROWS, :] = g[:, 128 * half : 128 * half + 128]
+
     def backward_change(t, pair, done):
         g_post, da = done
         g = g_post + jnp.dot(w_trans[...], da, preferred_element_type=F32)
         for i, z in enumerate(pair):
             cut = slice(PLANE * i, PLANE * i + PLANE)
-            if t > 0:
-                outgoing(z, g[:, cut], 5 - t)
-            else:
-                state[z] = g[:, cut]
+            outgoing(z, g[:, cut], 5 - t)
 
     def grads(t):
         g_in = lax.dot_general(xs[t], dact[...], NT, preferred_element_type=F32)
@@ -377,13 +406,13 @@
             done = (pair, now)
         second(t, *done)
 
-    def forwards(t, before=None):
-        in_turn(forward_hidden, forward_change, t, MIDDLE + OUTER, before)
-
-    def backwards(t, before=None):
-        in_turn(backward_hidden, backward_change, t, MIDDLE + OUTER, before)
-
-    forwards(0)
+    def forwards(t, pairs, before=None):
+        in_turn(forward_hidden, forward_change, t, pairs, before)
+
+    def nothing(t, pair, done):
+        pass
+
+    forwards(0, OUTER)
     for copy in copies_in[6:8]:
         copy.wait()
     pl.semaphore_wait(barrier, len(peers))
@@ -397,19 +426,24 @@
         outgoing(z, loaded(back_in, z), 0)
     copy_0 = halo(0, -1)
     begin(copy_0)
-    forwards(1, copy_1)
+    forwards(0, MIDDLE)
+    forwards(1, MIDDLE + OUTER, copy_1)
     copy_2 = halo(2, 1)
     begin(copy_2)
-    forwards(2, copy_2)
-    backwards(2, copy_0)
+    end(copy_0)
+    for pair in MIDDLE + OUTER:
+        backward_ahead(pair)
+    end(copy_2)
+    forwards(2, OUTER)
     copy_3 = halo(3, -1)
     begin(copy_3)
+    forwards(2, MIDDLE)
     grads(2)
-    backwards(1, copy_3)
+    in_turn(backward_hidden, backward_change, 1, MIDDLE + OUTER, copy_3)
     copy_4 = halo(4, -1)
     begin(copy_4)
     grads(1)
-    backwards(0, copy_4)
+    in_turn(backward_hidden, nothing, 0, MIDDLE + OUTER, copy_4)
     grads(0)
 
     def two(v):
@@ -447,9 +481,8 @@
     swap = remote(parts.at[pl.ds(other, 16)], from_core, core_send.at[0], core_recv.at[0], partner)
     swap.start()
 
-    for half in range(2):
-        for z in range(CZ):
-            start[half, ROWS * z : ROWS * z + ROWS, :] = state[z, :, 128 * half : 128 * half + 128]
+    for pair in MIDDLE + OUTER:
+        backward_field(pair)
     for half in range(2):
         for row in range(Q):
             by_q[0, WHERE[row], :, 128 * half : 128 * half + 128] = start[half, pl.ds(row, CZ, stride=ROWS), :]
@@ -460,7 +493,8 @@
     merged[...] = parts[pl.ds(mine, 16)] + from_core[...]
     per = 16 // ny
     scatter = []
-    for k in range(ny - 1, 0, -1):
+    y_far_first = sorted(range(1, ny), key=lambda k: -min(k, ny - k))
+    for k in y_far_first:
         piece = lax.rem(me_y + k, ny) * per
         scatter.append(remote(merged.at[pl.ds(piece, per)], from_y.at[k - 1], y_send.at[k - 1], y_recv.at[k - 1], at_y(k)))
     begin(scatter)
@@ -492,17 +526,24 @@
 
     own = pl.ds(core * 16 + me_y * per, per)
     final[own] = total * scale
-    spread_out = [
-        remote(final.at[own], final.at[own], e_send.at[k - 1], e_recv.at[k - 1], at_y(k)) for k in range(ny - 1, 0, -1)
-    ]
-    begin(spread_out)
-    end(spread_out)
-    give = remote(final.at[pl.ds(mine, 16)], final.at[pl.ds(mine, 16)], core_send.at[1], core_recv.at[1], partner)
-    give.start()
-    give.wait_recv()
+    def passed(k):
+        return pl.ds(core * 16 + lax.rem(me_y + ny - k, ny) * per, per)
+
+    spread_out = {
+        k: remote(final.at[own], final.at[own], e_send.at[k - 1], e_recv.at[k - 1], at_y(k)) for k in y_far_first
+    }
+    begin(spread_out.values())
+    give = {
+        k: remote(final.at[passed(k)], final.at[passed(k)], g_send.at[k], g_recv.at[k], partner) for k in range(ny)
+    }
+    give[0].start()
+    for k in sorted(range(1, ny), key=lambda k: min(k, ny - k)):
+        spread_out[k].wait_recv()
+        give[k].start()
+    end(give.values())
     sums_out = pltpu.make_async_copy(final, sums, out_sem.at[1])
     sums_out.start()
-    for copies in (copy_0, copy_1, copy_2, copy_3, copy_4, [swap], scatter, across, along, spread_out, [give]):
+    for copies in (copy_0, copy_1, copy_2, copy_3, copy_4, [swap], scatter, across, along, spread_out.values(), give.values()):
         for copy in copies:
             copy.wait_send()
     field_out.wait()
@@ -578,6 +619,7 @@
                 pltpu.VMEM((STEPS, 128, CELLS), BF16),
                 pltpu.VMEM((STEPS, HID, CELLS), BF16),
                 pltpu.VMEM((HID, CELLS), BF16),
+                pltpu.VMEM((HID, CELLS), BF16),
                 pltpu.VMEM((48, CELLS), BF16),
                 pltpu.VMEM((HID, 128), BF16),
                 pltpu.VMEM((ROWS, HID), BF16),
@@ -596,6 +638,7 @@
                 pltpu.VMEM((32, 8, 128), F32),
                 dma((5, 4)), dma((5, 4)), dma((2,)), dma((2,)), dma((ny - 1,)), dma((ny - 1,)),
                 dma((max(nx - 1, 1),)), dma((max(nx - 1, 1),)), dma((nz - 1,)), dma((nz - 1,)), dma((ny - 1,)), dma((ny - 1,)),
+                dma((ny,)), dma((ny,)),
             ],
             compiler_params=pltpu.CompilerParams(collective_id=0, has_side_effects=True, vmem_limit_bytes=62 << 20),
             name="adjoint",

time: 63.4 us -> 62.1 us (0.979)
  Pallas kernels: 62.5 us -> 61.3 us
    pallas_call x1, Pallas kernels: 60.7 us -> 59.4 us  [per_device(): pl.pallas_call(body, out_shape=(jax.ShapeDtypeStruct(field.shape, F32), j...]
where the time goes in v3:
time: 62.1 us; the launch traced here: 61.9 us
  Pallas kernels  61.3 us (99%)
  between operations  0.64 us (1%)
    pallas_call x1, Pallas kernels, per_device(): pl.pallas_call(body, out_shape=(jax.ShapeDtypeStruct(field.shape, F32), j...  59.4 us
    pallas_call x1, Pallas kernels, per_device(): pl.pallas_call(write_out, out_shape=(jax.ShapeDtypeStruct(field.shape, F3...  1.82 us

profile of v3, /device:TPU:1, one launch (start us, length us, event | category | flops | bytes accessed | tf_op | source)
XLA Modules:
  0.0 61.9 jit_solution(2499952949058092635)
XLA Ops:
  0.6 59.4 %adjoint.1 = (f32[1,39,8,256]{3,2,1,0:T(8,128)}, f32[32,8,128]{2,1,0:T(8,128)}) custom-call(f32[1,39,8,256]{3,2,1,0:T(8,128)} %refs_0_.1, s32[1,8,256]{2,1,0:T(8,128)} %refs_1_.1, f32[1,39,8,256]{3,2,1,0:T(8,128)} %refs_2_.1, bf16[20,512]{1,0:T(8,128)(2,1)} %refs_3_.1, f32[1,512]{1,0:T(1,128)} %bitcast.7, bf16[39,512]{1,0:T(8,128)(2,1)} %bitcast.6, ...), custom_call_target="tpu_custom_call" | custom-call | tf_op jit(solution)/shard_map/adjoint/pallas_call | solution.py:595
  60.1 1.8 %write_out.1 = (f32[1,39,8,256]{3,2,1,0:T(8,128)}, f32[20,512]{1,0:T(8,128)}, f32[1,512]{1,0:T(1,128)}, f32[39,512]{1,0:T(8,128)}, f32[1,39]{1,0:T(1,128)}) custom-call(f32[1,39,8,256]{3,2,1,0:T(8,128)} %get-tuple-element.12.field_at, f32[32,8,128]{2,1,0:T(8,128)} %get-tuple-element.13.sums_at), custom_call_target="tpu_custom_call" | custom-call | tf_op jit(solution)/shard_map/write_out/pallas_call | solution.py:646

commit v4 on v3

--- a/solution.py
+++ b/solution.py
@@ -136,8 +136,8 @@
     (
     field_at, solid_at, cotangent_at, w_in_at, b_in_at, w_out_at, b_out_at, floats_at, ints_at, d_field, sums,
     field, solid, cotangent, w_in, b_in, w_out, b_out, floats, ints, by_q, in_sem, out_sem, pads, start, back_in, state, bounce, walls, xs, hid, dact, dhs, gbs, w_stack, w_trans, wo, wo_trans, bias, acc_in, acc_out,
-    acc_b, parts, from_core, from_y, from_x, from_z, merged, final,
-    halo_send, halo_recv, core_send, core_recv, y_send, y_recv, x_send, x_recv, z_send, z_recv, e_send, e_recv, g_send, g_recv,
+    acc_b, parts, from_core, from_xy, from_z, merged, final,
+    halo_send, halo_recv, core_send, core_recv, xy_send, xy_recv, z_send, z_recv, e_send, e_recv, g_send, g_recv,
     ) = refs
     ny, nz, nx = grid
     me_s, me_x = lax.axis_index("space"), lax.axis_index("traj")
@@ -149,14 +149,12 @@
     down = (lax.rem(me_s + n_space - 1, n_space), me_x)
     place = lambda y, z, c: (y * nz + z) * 2 + c
     partner = (place(me_y, me_z, 1 - core), me_x)
-    at_y = lambda k: (place(lax.rem(me_y + k, ny), me_z, core), me_x)
+    at = lambda dy, dx: (place(lax.rem(me_y + dy, ny), me_z, core), lax.rem(me_x + dx, nx))
     at_z = lambda k: (place(me_y, lax.rem(me_z + k, nz), core), me_x)
-    at_x = lambda k: (me_s, lax.rem(me_x + k, nx))
-    peers = [up, down] + [at_y(k) for k in range(1, ny)] + [at_x(k) for k in range(1, nx)] + [at_z(k) for k in range(1, nz)]
-
-    barrier = pltpu.get_barrier_semaphore()
-    for peer in peers:
-        pl.semaphore_signal(barrier, inc=1, device_id=peer, device_id_type=MESH)
+    hops = lambda k, n: min(k, n - k)
+    others = [(dy, dx) for dy in range(ny) for dx in range(nx) if dy or dx]
+    others.sort(key=lambda d: -hops(d[0], ny) - hops(d[1], nx))
+    peers = [up, down] + [at(*d) for d in others] + [at_z(k) for k in range(1, nz)]
 
     copies_in = [
         pltpu.make_async_copy(src, dst, in_sem.at[i])
@@ -169,6 +167,10 @@
     ]
     for copy in copies_in:
         copy.start()
+    barrier = pltpu.get_barrier_semaphore()
+    for peer in peers:
+        pl.semaphore_signal(barrier, inc=1, device_id=peer, device_id_type=MESH)
+
     for copy in copies_in[:5]:
         copy.wait()
 
@@ -461,24 +463,23 @@
     line = lax.dot_general(jnp.ones((8, PLANE), BF16), pair, NT, preferred_element_type=F32)
     line = line + jnp.concatenate([line[:, 64:], line[:, :64]], axis=1)
     line = jnp.take_along_axis(line, ints[4, 0:8], axis=1, mode="promise_in_bounds")
-    for i in range(3):
-        for j in range(4):
-            parts[4 * i + j] = upper[8 * i : 8 * i + 8, 128 * j : 128 * j + 128]
-    for row in range(Q):
-        i, k = divmod(WHERE[row] + 24, 8)
-        for j in range(4):
-            parts[4 * i + j, k : k + 1, :] = acc_out[row : row + 1, 128 * j : 128 * j + 128]
+    parts[MOM + 1 : 24] = jnp.zeros((23 - MOM, 4, 128), F32)
     for j in range(4):
-        parts[28 + j, 7:8, :] = line[0:1] if j == 0 else jnp.zeros((1, 128), F32)
+        cut = slice(128 * j, 128 * j + 128)
+        for row in range(MOM + 1):
+            parts[row, j : j + 1, :] = upper[row : row + 1, cut]
+        for row in range(Q):
+            parts[24 + WHERE[row], j : j + 1, :] = acc_out[row : row + 1, cut]
+        parts[63, j : j + 1, :] = line[0:1] if j == 0 else jnp.zeros((1, 128), F32)
 
     def remote(src, dst, send, recv, to):
         return pltpu.make_async_remote_copy(
             src_ref=src, dst_ref=dst, send_sem=send, recv_sem=recv, device_id=to, device_id_type=MESH
         )
 
-    mine = pl.multiple_of(core * 16, 16)
-    other = pl.multiple_of((1 - core) * 16, 16)
-    swap = remote(parts.at[pl.ds(other, 16)], from_core, core_send.at[0], core_recv.at[0], partner)
+    mine = core * 32
+    other = 32 - mine
+    swap = remote(parts.at[pl.ds(other, 32)], from_core, core_send.at[0], core_recv.at[0], partner)
     swap.start()
 
     for pair in MIDDLE + OUTER:
@@ -490,28 +491,18 @@
     field_out = pltpu.make_async_copy(by_q, d_field, out_sem.at[0])
     field_out.start()
     swap.wait_recv()
-    merged[...] = parts[pl.ds(mine, 16)] + from_core[...]
-    per = 16 // ny
+    merged[...] = parts[pl.ds(mine, 32)] + from_core[...]
+    per = 32 // (ny * nx)
+    share = lambda dy, dx: (lax.rem(me_y + dy, ny) * nx + lax.rem(me_x + dx, nx)) * per
     scatter = []
-    y_far_first = sorted(range(1, ny), key=lambda k: -min(k, ny - k))
-    for k in y_far_first:
-        piece = lax.rem(me_y + k, ny) * per
-        scatter.append(remote(merged.at[pl.ds(piece, per)], from_y.at[k - 1], y_send.at[k - 1], y_recv.at[k - 1], at_y(k)))
+    for i, (dy, dx) in enumerate(others):
+        src = merged.at[pl.ds(share(dy, dx), per)]
+        scatter.append(remote(src, from_xy.at[i], xy_send.at[i], xy_recv.at[i], at(dy, dx)))
     begin(scatter)
     end(scatter)
-    total = merged[pl.ds(me_y * per, per)]
-    for k in range(ny - 1):
-        total = total + from_y[k]
-
-    from_x[me_x] = total
-    across = [
-        remote(from_x.at[me_x], from_x.at[me_x], x_send.at[k - 1], x_recv.at[k - 1], at_x(k)) for k in range(1, nx)
-    ]
-    begin(across)
-    end(across)
-    total = from_x[0]
-    for k in range(1, nx):
-        total = total + from_x[k]
+    total = merged[pl.ds(share(0, 0), per)]
+    for i in range(len(others)):
+        total = total + from_xy[i]
 
     from_z[me_z] = total
     far_first = sorted(range(1, nz), key=lambda k: -min(k, nz - k))
@@ -524,26 +515,24 @@
     for k in range(1, nz):
         total = total + from_z[k]
 
-    own = pl.ds(core * 16 + me_y * per, per)
+    own = pl.ds(mine + share(0, 0), per)
     final[own] = total * scale
-    def passed(k):
-        return pl.ds(core * 16 + lax.rem(me_y + ny - k, ny) * per, per)
-
-    spread_out = {
-        k: remote(final.at[own], final.at[own], e_send.at[k - 1], e_recv.at[k - 1], at_y(k)) for k in y_far_first
-    }
-    begin(spread_out.values())
-    give = {
-        k: remote(final.at[passed(k)], final.at[passed(k)], g_send.at[k], g_recv.at[k], partner) for k in range(ny)
-    }
-    give[0].start()
-    for k in sorted(range(1, ny), key=lambda k: min(k, ny - k)):
-        spread_out[k].wait_recv()
-        give[k].start()
-    end(give.values())
+    spread_out = [
+        remote(final.at[own], final.at[own], e_send.at[i], e_recv.at[i], at(dy, dx)) for i, (dy, dx) in enumerate(others)
+    ]
+    begin(spread_out)
+    give = []
+    for k in sorted(range(ny), key=lambda k: hops(k, ny)):
+        for i, (dy, dx) in enumerate(others):
+            if dy == k:
+                spread_out[i].wait_recv()
+        line_of_x = final.at[pl.ds(mine + lax.rem(me_y + ny - k, ny) * nx * per, nx * per)]
+        give.append(remote(line_of_x, line_of_x, g_send.at[k], g_recv.at[k], partner))
+        give[-1].start()
+    end(give)
     sums_out = pltpu.make_async_copy(final, sums, out_sem.at[1])
     sums_out.start()
-    for copies in (copy_0, copy_1, copy_2, copy_3, copy_4, [swap], scatter, across, along, spread_out.values(), give.values()):
+    for copies in (copy_0, copy_1, copy_2, copy_3, copy_4, [swap], scatter, along, spread_out, give):
         for copy in copies:
             copy.wait_send()
     field_out.wait()
@@ -558,14 +547,12 @@
     sums_in.wait()
     for j in range(4):
         cut = slice(128 * j, 128 * j + 128)
-        a[0:8, cut] = sums[j]
-        a[8:16, cut] = sums[4 + j]
-        a[16:20, cut] = sums[8 + j, 0:4]
-        b[:, cut] = sums[8 + j, 4:5]
-        for i in range(3, 7):
-            c[8 * i - 24 : 8 * i - 16, cut] = sums[4 * i + j]
-        c[32:39, cut] = sums[28 + j, 0:7]
-    d[...] = sums[28, 7:8, 0:Q]
+        for row in range(MOM):
+            a[row : row + 1, cut] = sums[row, j : j + 1, :]
+        b[:, cut] = sums[MOM, j : j + 1, :]
+        for row in range(Q):
+            c[row : row + 1, cut] = sums[24 + row, j : j + 1, :]
+    d[...] = sums[63, 0:1, 0:Q]
     small = [
         pltpu.make_async_copy(src, dst, sem.at[i])
         for i, (src, dst) in enumerate([(a, g_w_in), (b, g_b_in), (c, g_w_out), (d, g_b_out)], 2)
@@ -584,7 +571,7 @@
     ny = 8 if n_space % 16 == 0 else 2
     nz = n_space // (2 * ny)
     scale = 1.0 / math.sqrt(float(n_space * nx * CELLS * STEPS))
-    per = 16 // ny
+    per = 32 // (ny * nx)
     hbm = pl.BlockSpec(memory_space=pltpu.HBM)
     dma = pltpu.SemaphoreType.DMA
 
@@ -594,7 +581,7 @@
 
         d_field, sums = pl.pallas_call(
             body,
-            out_shape=(jax.ShapeDtypeStruct(field.shape, F32), jax.ShapeDtypeStruct((32, 8, 128), F32)),
+            out_shape=(jax.ShapeDtypeStruct(field.shape, F32), jax.ShapeDtypeStruct((64, 4, 128), F32)),
             in_specs=[hbm] * 9,
             out_specs=(hbm, hbm),
             scratch_shapes=[
@@ -629,16 +616,14 @@
                 pltpu.VMEM((128, HID), F32),
                 pltpu.VMEM((48, HID), F32),
                 pltpu.VMEM((ROWS, PLANE), F32),
-                pltpu.VMEM((32, 8, 128), F32),
-                pltpu.VMEM((16, 8, 128), F32),
-                pltpu.VMEM((ny - 1, per, 8, 128), F32),
-                pltpu.VMEM((nx, per, 8, 128), F32),
-                pltpu.VMEM((nz, per, 8, 128), F32),
-                pltpu.VMEM((16, 8, 128), F32),
-                pltpu.VMEM((32, 8, 128), F32),
-                dma((5, 4)), dma((5, 4)), dma((2,)), dma((2,)), dma((ny - 1,)), dma((ny - 1,)),
-                dma((max(nx - 1, 1),)), dma((max(nx - 1, 1),)), dma((nz - 1,)), dma((nz - 1,)), dma((ny - 1,)), dma((ny - 1,)),
-                dma((ny,)), dma((ny,)),
+                pltpu.VMEM((64, 4, 128), F32),
+                pltpu.VMEM((32, 4, 128), F32),
+                pltpu.VMEM((ny * nx - 1, per, 4, 128), F32),
+                pltpu.VMEM((nz, per, 4, 128), F32),
+                pltpu.VMEM((32, 4, 128), F32),
+                pltpu.VMEM((64, 4, 128), F32),
+                dma((5, 4)), dma((5, 4)), dma((2,)), dma((2,)), dma((ny * nx - 1,)), dma((ny * nx - 1,)),
+                dma((nz - 1,)), dma((nz - 1,)), dma((ny * nx - 1,)), dma((ny * nx - 1,)), dma((ny,)), dma((ny,)),
             ],
             compiler_params=pltpu.CompilerParams(collective_id=0, has_side_effects=True, vmem_limit_bytes=62 << 20),
             name="adjoint",
@@ -655,7 +640,7 @@
             in_specs=[hbm, hbm],
             out_specs=(hbm,) * 5,
             scratch_shapes=[
-                pltpu.VMEM(field.shape, F32), pltpu.VMEM((32, 8, 128), F32),
+                pltpu.VMEM(field.shape, F32), pltpu.VMEM((64, 4, 128), F32),
                 pltpu.VMEM((MOM, HID), F32), pltpu.VMEM((1, HID), F32), pltpu.VMEM((Q, HID), F32), pltpu.VMEM((1, Q), F32),
                 dma((7,)),
             ],

time: 62.1 us -> 62.3 us (level)
  no operation moved by 1% of the time
where the time goes in v4:
time: 62.3 us; the launch traced here: 62.2 us
  Pallas kernels  61.5 us (99%)
  between operations  0.64 us (1%)
    pallas_call x1, Pallas kernels, per_device(): pl.pallas_call(body, out_shape=(jax.ShapeDtypeStruct(field.shape, F32), j...  59.7 us
    pallas_call x1, Pallas kernels, per_device(): pl.pallas_call(write_out, out_shape=(jax.ShapeDtypeStruct(field.shape, F3...  1.82 us

profile of v4, /device:TPU:1, one launch (start us, length us, event | category | flops | bytes accessed | tf_op | source)
XLA Modules:
  0.0 62.2 jit_solution(6446687500703523509)
XLA Ops:
  0.6 59.7 %adjoint.1 = (f32[1,39,8,256]{3,2,1,0:T(8,128)}, f32[64,4,128]{2,1,0:T(4,128)}) custom-call(f32[1,39,8,256]{3,2,1,0:T(8,128)} %refs_0_.1, s32[1,8,256]{2,1,0:T(8,128)} %refs_1_.1, f32[1,39,8,256]{3,2,1,0:T(8,128)} %refs_2_.1, bf16[20,512]{1,0:T(8,128)(2,1)} %refs_3_.1, f32[1,512]{1,0:T(1,128)} %bitcast.7, bf16[39,512]{1,0:T(8,128)(2,1)} %bitcast.6, ...), custom_call_target="tpu_custom_call" | custom-call | tf_op jit(solution)/shard_map/adjoint/pallas_call | solution.py:582
  60.3 1.8 %write_out.1 = (f32[1,39,8,256]{3,2,1,0:T(8,128)}, f32[20,512]{1,0:T(8,128)}, f32[1,512]{1,0:T(1,128)}, f32[39,512]{1,0:T(8,128)}, f32[1,39]{1,0:T(1,128)}) custom-call(f32[1,39,8,256]{3,2,1,0:T(8,128)} %get-tuple-element.12.field_at, f32[64,4,128]{2,1,0:T(4,128)} %get-tuple-element.13.sums_at), custom_call_target="tpu_custom_call" | custom-call | tf_op jit(solution)/shard_map/write_out/pallas_call | solution.py:631
